TPU v7x, 32 devices: a whole 2x2x4 slice. The times are simulated.
32 devices in a mesh: group: 4 (over y, core), span: 8 (over z, x).
Axes of the slice: x: 2, y: 2, z: 4, core: 2. Of those that a mesh axis runs over, the one named last changes fastest.
Arguments:
- tokens: bfloat16 [4096, 1024], P(('group', 'span')), may hold values from -32 to 32
- query_weight: bfloat16 [1024, 1024], replicated, may hold values from -0.1875 to 0.1875
- key_weight: bfloat16 [1024, 1024], replicated, may hold values from -0.1875 to 0.1875
- value_weight: bfloat16 [1024, 1024], replicated, may hold values from -0.1875 to 0.1875
- log_decay: float32 [16, 4096], P(None, ('group', 'span')), may hold values from -0.6 to 0
- neighbour_blocks: int32 [32, 4], P(('group', 'span')), may hold values from 0 to 31, as said below
- cotangent: bfloat16 [4096, 1024], P(('group', 'span')), may hold values from -6 to 6
Outputs:
- layer_out: bfloat16 [4096, 1024], P(('group', 'span'))
- tokens_grad: bfloat16 [4096, 1024], P(('group', 'span'))
- query_grad: bfloat16 [1024, 1024], replicated
- key_grad: bfloat16 [1024, 1024], replicated
- value_grad: bfloat16 [1024, 1024], replicated
Inputs may be any that keep to these rules, and one draw needn't show every extreme that they name: `neighbour_blocks`: row b is [b, b - 1, b - 1, b - 1]; any entry that would fall before block 0 is block 0.
All inputs are finite; a program needn't handle non-finite values.
Results may differ from a plain program's by a relative error of at most 0.0077.
Values may be sent and summed in bfloat16 or wider, within the bound.
A program may use at most 192 MiB of HBM per device.

v0:
```python
import math

import jax
import jax.numpy as jnp
from jax import lax
from jax.sharding import PartitionSpec as P

BLK = 128
NB = 4


def prefix(part, axis, combine, identity, reverse):
    count = lax.axis_size(axis)
    place = lax.axis_index(axis)
    ahead = count - 1 - place if reverse else place
    gathered = jax.tree.map(lambda a: lax.all_gather(a, axis), part)
    state = jax.tree.map(lambda a, e: jnp.zeros_like(a) + jnp.asarray(e, a.dtype), part, identity)

    def one(hop, state):
        source = count - 1 - hop if reverse else hop
        return combine(
            state, jax.tree.map(lambda a: lax.dynamic_index_in_dim(a, source, 0, False), gathered)
        )

    return lax.fori_loop(0, ahead, one, state)


def shifted(block, axis, distance):
    devices = range(lax.axis_size(axis))
    route = [(i - distance, i) for i in devices if i - distance in devices]
    return lax.ppermute(block, axis, route)


def project(inputs, weight):
    return jnp.dot(inputs, weight, preferred_element_type=jnp.float32).astype(jnp.bfloat16)


def back_project(grad_kv, key_weight, value_weight, feat_width):
    key_part = jnp.einsum(
        "tc,dc->td", grad_kv[:, :feat_width], key_weight, preferred_element_type=jnp.float32
    )
    return key_part + jnp.einsum(
        "tc,dc->td", grad_kv[:, feat_width:], value_weight, preferred_element_type=jnp.float32
    )


def join_carry(earlier, later):
    return (earlier[0] + later[0], jnp.exp(later[0])[:, None] * earlier[1] + later[1])


def carry_across(seg_total, seg_state, reverse):
    identity_pair = (jnp.zeros_like(seg_total), jnp.zeros_like(seg_state))
    result = prefix((seg_total, seg_state), ("group", "span"), join_carry, identity_pair, reverse)
    return result[1]


def shards(tokens, query_weight, key_weight, value_weight, log_decay, neighbour_blocks, cotangent):
    row_count, feat_width = tokens.shape
    head_count = log_decay.shape[0]
    head_size = feat_width // head_count
    blocks = row_count // BLK
    lin_scale = 1.0 / (head_size * math.sqrt(row_count))
    soft_scale = 1.0 / math.sqrt(head_size)
    devices = lax.axis_size(("group", "span"))
    position = lax.axis_index(("group", "span"))
    query = project(tokens, query_weight)
    keyval = jnp.concatenate([project(tokens, key_weight), project(tokens, value_weight)], axis=1)
    running = jnp.cumsum(log_decay, axis=1)
    seg_total = running[:, -1]
    growth = jnp.exp(running).T[:, :, None]
    fading = jnp.exp(seg_total[:, None] - running).T[:, :, None]
    q_heads = query.reshape(row_count, head_count, head_size)
    k_heads = keyval[:, :feat_width].reshape(row_count, head_count, head_size)
    v_heads = keyval[:, feat_width:].reshape(row_count, head_count, head_size)
    g_heads = cotangent.reshape(row_count, head_count, head_size)
    weighted = (v_heads * fading).astype(jnp.bfloat16)
    local_state = jnp.einsum(
        "shd,she->hde", k_heads, weighted, preferred_element_type=jnp.float32
    ).reshape(head_count, head_size * head_size)
    scaled_grad = (g_heads * growth).astype(jnp.bfloat16)
    head_grad = lin_scale * jnp.einsum(
        "thd,the->hde", q_heads, scaled_grad, preferred_element_type=jnp.float32
    )
    head_grad = head_grad.reshape(head_count, head_size * head_size)
    state_in = carry_across(seg_total, local_state, False).reshape(head_count, head_size, head_size)
    later = carry_across(seg_total, head_grad, True).reshape(head_count, head_size, head_size)
    prev_tokens = shifted(tokens, ("group", "span"), 1)
    prev_keyval = jnp.concatenate(
        [project(prev_tokens, key_weight), project(prev_tokens, value_weight)], axis=1
    )
    places = jnp.arange(row_count, dtype=jnp.int32)
    is_lower = places[:, None] >= places[None, :]
    decay_mat = jnp.where(
        is_lower[None], jnp.exp(jnp.minimum(running[:, :, None] - running[:, None, :], 0.0)), 0.0
    )
    intra_mat = (
        jnp.einsum("thd,shd->hts", q_heads, k_heads, preferred_element_type=jnp.float32) * decay_mat
    ).astype(jnp.bfloat16)
    state_bf = state_in.astype(jnp.bfloat16)
    linear_out = jnp.einsum("hts,she->the", intra_mat, v_heads, preferred_element_type=jnp.float32)
    linear_out = linear_out + growth * jnp.einsum(
        "thd,hde->the", q_heads, state_bf, preferred_element_type=jnp.float32
    )
    extended = jnp.concatenate([prev_keyval, keyval], axis=0).reshape(
        2 * blocks, BLK, 2 * feat_width
    )
    local_ids = neighbour_blocks - (position - 1) * blocks
    picked = jnp.take(extended, local_ids, axis=0).reshape(blocks, NB * BLK, 2 * feat_width)
    near_key = picked[:, :, :feat_width].reshape(blocks, NB * BLK, head_count, head_size)
    near_val = picked[:, :, feat_width:].reshape(blocks, NB * BLK, head_count, head_size)
    q_blocks = q_heads.reshape(blocks, BLK, head_count, head_size)
    g_blocks = g_heads.reshape(blocks, BLK, head_count, head_size)
    logits = (
        jnp.einsum("bthd,bshd->bhts", q_blocks, near_key, preferred_element_type=jnp.float32)
        * soft_scale
    )
    row_peak = jnp.max(logits, axis=-1, keepdims=True)
    exp_terms = jnp.exp(logits - row_peak)
    soft_probs = exp_terms / jnp.sum(exp_terms, axis=-1, keepdims=True)
    probs_bf = soft_probs.astype(jnp.bfloat16)
    near_out = jnp.einsum(
        "bhts,bshd->bthd", probs_bf, near_val, preferred_element_type=jnp.float32
    ).reshape(row_count, head_count, head_size)
    layer_out = (
        (lin_scale * linear_out + near_out).reshape(row_count, feat_width).astype(jnp.bfloat16)
    )
    prob_grad = jnp.einsum(
        "bthd,bshd->bhts", g_blocks, near_val, preferred_element_type=jnp.float32
    )
    inner_sum = jnp.sum(soft_probs * prob_grad, axis=-1, keepdims=True)
    dlogit = (soft_probs * (prob_grad - inner_sum) * soft_scale).astype(jnp.bfloat16)
    dq_near = jnp.einsum(
        "bhts,bshd->bthd", dlogit, near_key, preferred_element_type=jnp.float32
    ).reshape(row_count, head_count, head_size)
    dk_near = jnp.einsum(
        "bhts,bthd->bshd", dlogit, q_blocks, preferred_element_type=jnp.float32
    ).reshape(blocks * NB, BLK, feat_width)
    dv_near = jnp.einsum(
        "bhts,bthd->bshd", probs_bf, g_blocks, preferred_element_type=jnp.float32
    ).reshape(blocks * NB, BLK, feat_width)
    dpicked = jnp.concatenate([dk_near, dv_near], axis=-1)
    onehot = (
        local_ids.reshape(-1)[:, None] == jnp.arange(2 * blocks, dtype=jnp.int32)[None, :]
    ).astype(jnp.float32)
    ext_grad = jnp.einsum("nm,ntc->mtc", onehot, dpicked, precision=lax.Precision.HIGHEST).reshape(
        2 * row_count, 2 * feat_width
    )
    back_mat = (
        jnp.einsum("thd,shd->hts", g_heads, v_heads, preferred_element_type=jnp.float32) * decay_mat
    ).astype(jnp.bfloat16)
    later_bf = later.astype(jnp.bfloat16)
    dq_lin = jnp.einsum("hts,shd->thd", back_mat, k_heads, preferred_element_type=jnp.float32)
    dq_lin = lin_scale * (
        dq_lin
        + growth * jnp.einsum("the,hde->thd", g_heads, state_bf, preferred_element_type=jnp.float32)
    )
    dk_lin = lin_scale * jnp.einsum(
        "hts,thd->shd", back_mat, q_heads, preferred_element_type=jnp.float32
    )
    dk_lin = dk_lin + fading * jnp.einsum(
        "she,hde->shd", v_heads, later_bf, preferred_element_type=jnp.float32
    )
    dv_lin = lin_scale * jnp.einsum(
        "hts,the->she", intra_mat, g_heads, preferred_element_type=jnp.float32
    )
    dv_lin = dv_lin + fading * jnp.einsum(
        "shd,hde->she", k_heads, later_bf, preferred_element_type=jnp.float32
    )
    query_delta = (dq_lin + dq_near).reshape(row_count, feat_width).astype(jnp.bfloat16)
    lin_kv = jnp.concatenate(
        [dk_lin.reshape(row_count, feat_width), dv_lin.reshape(row_count, feat_width)], axis=1
    )
    own_grad = (lin_kv + ext_grad[row_count:]).astype(jnp.bfloat16)
    prev_grad = ext_grad[:row_count].astype(jnp.bfloat16)
    query_part = jnp.einsum("td,tc->dc", tokens, query_delta, preferred_element_type=jnp.float32)
    kv_part = jnp.einsum("td,tc->dc", tokens, own_grad, preferred_element_type=jnp.float32)
    tokens_back = jnp.einsum(
        "tc,dc->td", query_delta, query_weight, preferred_element_type=jnp.float32
    )
    tokens_back = tokens_back + back_project(own_grad, key_weight, value_weight, feat_width)
    kv_part = kv_part + jnp.einsum(
        "td,tc->dc", prev_tokens, prev_grad, preferred_element_type=jnp.float32
    )
    owed_back = back_project(prev_grad, key_weight, value_weight, feat_width)
    tokens_back = tokens_back + shifted(
        owed_back.astype(jnp.bfloat16), ("group", "span"), -1
    ).astype(owed_back.dtype)
    grad_norm = 1.0 / math.sqrt(row_count * devices)
    key_part = kv_part[:, :feat_width]
    value_part = kv_part[:, feat_width:]
    summed = lax.psum((query_part, key_part, value_part), ("group", "span"))
    weight_grads = tuple(((part_sum * grad_norm).astype(jnp.bfloat16) for part_sum in summed))
    return (
        layer_out,
        tokens_back.astype(jnp.bfloat16),
        weight_grads[0],
        weight_grads[1],
        weight_grads[2],
    )


def solution(mesh):
    return jax.shard_map(
        shards,
        mesh=mesh,
        in_specs=(
            P(("group", "span"), None),
            P(),
            P(),
            P(),
            P(None, ("group", "span")),
            P(("group", "span"), None),
            P(("group", "span"), None),
        ),
        out_specs=(P(("group", "span"), None), P(("group", "span"), None), P(), P(), P()),
        check_vma=False,
    )
```

profile of v0, /device:TPU:0, one launch (start us, length us, event | category | flops | bytes accessed | tf_op | source)
XLA Modules:
  0.0 523.2 jit_solution(16642835467970692131)
XLA Ops:
  7.2 1.1 reduce_window_sum.11
  8.6 1.1 copy.62
  9.8 2.2 convolution_convert_fusion.3
  13.4 2.0 convolution_convert_fusion.4
  16.2 1.1 convolution_convert_fusion.2
  17.4 1.1 copy.59
  18.5 1.1 fusion.44
  19.6 1.9 all_gather_reshape.6
  21.5 5.6 %collective-permute-start = (bf16[128,1024]{1,0:T(8,128)(2,1)S(1)}, bf16[128,1024]{1,0:T(8,128)(2,1)}, u32[]{:S(2)}, u32[]{:S(2)}) collective-permute-start(bf16[128,1024]{1,0:T(8,128)(2,1)S(1)} %copy-done.3), channel_id=1, source_target_pairs={{0,1},{1,2},{2,3},{3,4},{4,5},{5,6},{6,7},{7,8},{8,9},{9,10},{10,1... | collective-permute-start | bytes 786440 | tf_op jit(solution)/shard_map/ppermute | solution.py:31
  27.3 1.3 fusion.18
  29.2 1.1 fusion.35
  30.3 1.3 convolution_bitcast_fusion.6
  31.8 41.6 %all-reduce = f32[512]{0:T(512)S(1)} all-reduce(f32[512]{0:T(512)S(1)} %dynamic-update-slice), channel_id=2, replica_groups=mesh['group'=4,'span'=8] {'group','span'}, use_global_device_ids=true, to_apply=%add | all-reduce | flops 512 | bytes 4096
  73.5 2.1 fusion.34
  75.6 2.1 convolution_convert_fusion
  77.8 1.4 convolution_convert_fusion.1
  79.2 1.1 maximum_maximum_fusion
  80.3 2.0 gather_fusion
  82.3 4.0 copy.61
  86.2 1.8 broadcast_select_fusion
  88.1 1.5 fusion.66
  89.6 4.5 fusion.67
  94.1 4.1 convolution_bitcast_fusion.1
  98.2 2.9 reshape.204
  101.1 3.9 copy.69
  105.0 4.0 fusion.68
  109.1 18.8 %fusion.16 = f32[1,512,16,64]{1,3,2,0:T(8,128)} fusion(bf16[128,16,64]{0,2,1:T(8,128)(2,1)S(1)} %bitcast.227, f32[16,512,128]{1,2,0:T(8,128)} %fusion.68, f32[16,128,512]{2,1,0:T(8,128)} %get-tuple-element.182, f32[16,128]{1,0:T(8,128)S(1)} %get-tuple-element.181), kind=kOutput, calls=%fused_computation.30 | convolution fusion | flops 141560320 | bytes 10756096 | tf_op jit(solution)/shard_map/bhts,bthd->bshd/dot_general | solution.py:135
  127.9 2.9 reshape.203
  130.8 4.0 copy.68
  134.8 6.8 %fusion.2 = f32[2,128,2048]{2,0,1:T(2,128)S(1)} fusion(f32[4,128,1024]{2,0,1:T(4,128)} %copy.69, f32[4,128,1024]{2,0,1:T(4,128)} %copy.68, s32[4]{0:T(128)S(1)} %subtract_bitcast_fusion), kind=kOutput, calls=%fused_computation.8 | convolution fusion | flops 26214408 | bytes 6291472 | tf_op jit(solution)/shard_map/nm,ntc->mtc/dot_general | solution.py:145
  142.6 2.1 slice.55
  144.6 1.1 copy.82
  145.8 34.4 %while.27 = (s32[]{:T(128)}, f32[16,4096]{1,0:T(8,128)S(1)}, s32[]{:T(128)}, f32[32,16]{1,0:T(8,128)S(1)}, f32[32,16,4096]{2,1,0:T(8,128)}, /*index=5*/s32[]{:T(128)}, s32[]{:T(128)}, s32[]{:T(128)}, s32[]{:T(128)}) while((s32[]{:T(128)}, f32[16,4096]{1,0:T(8,128)S(1)}, s32[]{:T(128)}, f32[32,16]{1,0:T(8,128)S(1)}, f32[32,16,4096]{2,1,0:T(8,128)}, ...), condition=%wide.region_7.8_spmd, body=%wide.region_6.7_spmd.sunk | while | flops 131078 | bytes 786779 | solution.py:25
  152.4 1.1 bitcast_add_fusion.5
  155.8 1.1 bitcast_add_fusion.5
  158.0 1.1 bitcast_add_fusion.5
  159.1 1.1 bitcast_add_fusion.5
  162.4 1.1 bitcast_add_fusion.5
  168.0 1.1 bitcast_add_fusion.5
  169.1 1.1 bitcast_add_fusion.5
  171.3 1.1 bitcast_add_fusion.5
  181.0 2.1 fusion.30
  183.1 2.1 copy.66
  185.2 2.2 fusion.32
  187.3 2.1 copy.67
  189.9 2.1 fusion.28
  192.1 17.8 %fusion.37 = bf16[128,16,64]{0,2,1:T(8,128)(2,1)S(1)} fusion(f32[128,16,64]{0,2,1:T(8,128)} %fusion.28, bf16[512,16,64]{0,2,1:T(8,128)(2,1)} %bitcast.249, f32[16,512,128]{1,2,0:T(8,128)} %fusion.68, f32[16,128,512]{2,1,0:T(8,128)} %get-tuple-element.182, f32[16,128]{1,0:T(8,128)S(1)} %copy-done.26), kind=kOutput, calls=%fused_computation.66 | convolution fusion | flops 141822464 | bytes 10231808 | tf_op jit(solution)/shard_map/bhts,bshd->bthd/dot_general | solution.py:132
  210.6 2.6 convolution_bitcast_fusion
  213.7 1.3 fusion.70
  215.0 2.2 add_bitcast_fusion
  217.2 4.1 fusion.65
  222.3 1.6 convolution_bitcast_fusion.9
  223.9 2.6 fusion.46
  226.5 1.5 fusion.38
  228.1 1.5 collective-permute-start.1
  231.7 2.6 fusion.69
  235.1 2.6 collective-permute-done.1
  237.7 2.5 add_convert_fusion
  240.2 253.6 %all-reduce.4.cloned.1.call-done = (f32[1024,1024]{0,1:T(8,128)}, f32[1024,1024]{0,1:T(8,128)}, f32[1024,1024]{0,1:T(8,128)}) async-done(((f32[1024,1024]{0,1:T(8,128)}, f32[1024,1024]{0,1:T(8,128)}, f32[1024,1024]{0,1:T(8,128)}), (f32[1024,1024]{0,1:T(8,128)}, f32[1024,1024]{0,1:T(8,128)}, f32[1024,1024]{0,1:T(8,128)})) %all-reduce.4.cloned.1.call-update) | async-done | bytes 12582928 | tf_op jit(solution)/shard_map/psum | solution.py:191
  493.8 4.1 multiply_convert_fusion.2
  497.9 3.9 copy.71
  501.8 6.7 %multiply_convert_fusion = (bf16[1024,1024]{0,1:T(8,128)(2,1)}, bf16[1024,1024]{0,1:T(8,128)(2,1)}) fusion(f32[1024,1024]{0,1:T(8,128)} %get-tuple-element.172, f32[1024,1024]{0,1:T(8,128)} %get-tuple-element.171), kind=kLoop, calls=%fused_computation.17 | loop fusion | flops 4194304 | bytes 12582912 | tf_op jit(solution)/shard_map/convert_element_type | solution.py:192
  508.6 3.9 copy.73
  512.5 3.9 copy.72
  (147 shorter events, 35.6 us)
Async XLA Ops:
  7.2 9.0 %copy-start = (bf16[1024,1024]{1,0:T(8,128)(2,1)S(1)}, bf16[1024,1024]{1,0:T(8,128)(2,1)}, u32[]{:S(2)}) copy-start(bf16[1024,1024]{1,0:T(8,128)(2,1)} %param.13) | copy-start | bytes 6291460
  7.2 6.3 %copy-start.3 = (bf16[128,1024]{1,0:T(8,128)(2,1)S(1)}, bf16[128,1024]{1,0:T(8,128)(2,1)}, u32[]{:S(2)}) copy-start(bf16[128,1024]{1,0:T(8,128)(2,1)} %param.11) | copy-start | bytes 786436
  7.2 138.5 %all-gather.6.cloned.1.call-start = ((), (), s32[]{:S(2)}) async-start(), calls=%async_computation.1 | async-start | bytes 8650752 | tf_op jit(solution)/shard_map/all_gather | solution.py:16
  9.8 63.7 %copy-start.6 = (bf16[128,1024]{0,1:T(8,128)(2,1)}, bf16[128,1024]{0,1:T(8,128)(2,1)S(1)}, u32[]{:S(2)}) copy-start(bf16[128,1024]{0,1:T(8,128)(2,1)S(1)} %copy.62) | copy-start | bytes 786436
  12.2 17.0 %copy-start.4 = (bf16[128,1024]{0,1:T(8,128)(2,1)}, bf16[128,1024]{0,1:T(8,128)(2,1)S(1)}, u32[]{:S(2)}) copy-start(bf16[128,1024]{0,1:T(8,128)(2,1)S(1)} %copy.58) | copy-start | bytes 786436
  13.4 13.8 %copy-start.27 = (s32[1,4]{1,0:T(1,128)S(1)}, s32[1,4]{1,0:T(1,128)}, u32[]{:S(2)}) copy-start(s32[1,4]{1,0:T(1,128)} %param.16) | copy-start | bytes 52
  13.4 176.0 %all-gather.4.cloned.1.call-start = ((), (), s32[]{:S(2)}) async-start(), calls=%async_computation | async-start | bytes 8650752 | tf_op jit(solution)/shard_map/all_gather | solution.py:16
  15.5 0.7 copy-start.17
  16.2 13.0 %copy-start.12 = (bf16[128,1024]{0,1:T(8,128)(2,1)}, bf16[128,1024]{0,1:T(8,128)(2,1)S(1)}, u32[]{:S(2)}) copy-start(bf16[128,1024]{0,1:T(8,128)(2,1)S(1)} %copy.57) | copy-start | bytes 786436
  18.5 13.0 %copy-start.15 = (bf16[128,1024]{0,1:T(8,128)(2,1)}, bf16[128,1024]{0,1:T(8,128)(2,1)S(1)}, u32[]{:S(2)}) copy-start(bf16[128,1024]{0,1:T(8,128)(2,1)S(1)} %copy.59) | copy-start | bytes 786436
  21.5 472.3 %all-reduce.4.cloned.1.call-start = ((), (), s32[]{:S(2)}) async-start(), calls=%async_computation.2 | async-start | bytes 25165824 | tf_op jit(solution)/shard_map/psum | solution.py:191
  21.5 54.1 %collective-permute-start = (bf16[128,1024]{1,0:T(8,128)(2,1)S(1)}, bf16[128,1024]{1,0:T(8,128)(2,1)}, u32[]{:S(2)}, u32[]{:S(2)}) collective-permute-start(bf16[128,1024]{1,0:T(8,128)(2,1)S(1)} %copy-done.3), channel_id=1, source_target_pairs={{0,1},{1,2},{2,3},{3,4},{4,5},{5,6},{6,7},{7,8},{8,9},{9,10},{10,1... | collective-permute-start | bytes 786440 | tf_op jit(solution)/shard_map/ppermute | solution.py:31
  86.2 3.4 copy-start.5
  88.1 6.1 %copy-start.7 = (bf16[128,1024]{0,1:T(8,128)(2,1)S(1)}, bf16[128,1024]{0,1:T(8,128)(2,1)}, u32[]{:S(2)}) copy-start(bf16[128,1024]{0,1:T(8,128)(2,1)} %copy-done.6) | copy-start | bytes 786436
  94.1 14.9 %copy-start.25 = (f32[16,128]{1,0:T(8,128)}, f32[16,128]{1,0:T(8,128)S(1)}, u32[]{:S(2)}) copy-start(f32[16,128]{1,0:T(8,128)S(1)} %get-tuple-element.181) | copy-start | bytes 24580
  142.6 38.5 %copy-start.13 = (bf16[128,1024]{0,1:T(8,128)(2,1)S(1)}, bf16[128,1024]{0,1:T(8,128)(2,1)}, u32[]{:S(2)}) copy-start(bf16[128,1024]{0,1:T(8,128)(2,1)} %copy-done.12) | copy-start | bytes 786436
  180.2 0.6 copy-start.24
  187.3 4.7 copy-start.26
  189.9 19.9 %copy-start.18 = (bf16[16,64,64]{2,1,0:T(8,128)(2,1)}, bf16[16,64,64]{2,1,0:T(8,128)(2,1)S(1)}, u32[]{:S(2)}) copy-start(bf16[16,64,64]{2,1,0:T(8,128)(2,1)S(1)} %convert_element_type.98) | copy-start | bytes 393220
  209.9 0.7 copy-start.22
  209.9 3.3 copy-start.11
  209.9 3.3 copy-start.20
  209.9 3.3 copy-start.21
  213.7 1.3 copy-start.8
  221.3 0.9 copy-start.14
  221.3 8.3 %copy-start.19 = (bf16[16,64,64]{2,1,0:T(8,128)(2,1)S(1)}, bf16[16,64,64]{2,1,0:T(8,128)(2,1)}, u32[]{:S(2)}) copy-start(bf16[16,64,64]{2,1,0:T(8,128)(2,1)} %copy-done.18) | copy-start | bytes 393220
  222.2 4.2 copy-start.1
  222.2 4.3 copy-start.9
  222.3 7.6 %copy-start.10 = (f32[16,128,512]{2,1,0:T(8,128)S(1)}, f32[16,128,512]{2,1,0:T(8,128)}, u32[]{:S(2)}) copy-start(f32[16,128,512]{2,1,0:T(8,128)} %get-tuple-element.182) | copy-start | bytes 12582916
  222.3 7.6 %copy-start.16 = (bf16[1,512,1024]{1,2,0:T(8,128)(2,1)S(1)}, bf16[1,512,1024]{1,2,0:T(8,128)(2,1)}, u32[]{:S(2)}) copy-start(bf16[1,512,1024]{1,2,0:T(8,128)(2,1)} %get-tuple-element.178) | copy-start | bytes 3145732
  228.1 9.6 %collective-permute-start.1 = (bf16[128,1024]{1,0:T(8,128)(2,1)}, bf16[128,1024]{1,0:T(8,128)(2,1)}, u32[]{:S(2)}, u32[]{:S(2)}) collective-permute-start(bf16[128,1024]{1,0:T(8,128)(2,1)} %fusion.38), channel_id=1, source_target_pairs={{1,0},{2,1},{3,2},{4,3},{5,4},{6,5},{7,6},{8,7},{9,8},{10,9},{11,1... | collective-permute-start | bytes 786440 | tf_op jit(solution)/shard_map/ppermute | solution.py:31
  229.9 1.8 copy-start.23
  231.7 6.0 %copy-start.2 = (bf16[1024,1024]{1,0:T(8,128)(2,1)S(1)}, bf16[1024,1024]{1,0:T(8,128)(2,1)}, u32[]{:S(2)}) copy-start(bf16[1024,1024]{1,0:T(8,128)(2,1)} %param.14) | copy-start | bytes 6291460
Sparse Core Ops, SparseCore 0:
  13.5 82.0 all-gather.5
  98.6 75.8 all-gather.3
  221.4 272.3 all-reduce.3
where the time goes:
time: 530 us; the launch traced here: 523 us
  waiting for transfers between devices  256 us (48%)
  matrix products  98.1 us (19%)
  local copies, waits for them, and re-layouts  55.8 us (11%)
  other arithmetic  48.6 us (9%)
  blocking collectives  41.6 us (8%)
  between operations  14.5 us (3%)
  starting transfers between devices  7.23 us (1%)
    psum x1, waiting for transfers between devices, shards(): summed = lax.psum((query_part, key_part, value_part), ('group', 'span'))  254 us
    unnamed x1, blocking collectives  41.6 us
    add x31, other arithmetic, join_carry(): jnp.exp(later[0])[:, None] * earlier[1] + later[1]  33.1 us
    dot_general x1, matrix products, shards(): jnp.einsum('bhts,bthd->bshd', dlogit, q_blocks, preferred_element_type=jn...  18.8 us
    unnamed x64, local copies, waits for them, and re-layouts  17.9 us
    dot_general x1, matrix products, shards(): jnp.einsum('bhts,bshd->bthd', dlogit, near_key, preferred_element_type=jn...  17.8 us
    convert_element_type x2, other arithmetic, shards(): (part_sum * grad_norm).astype(jnp.bfloat16)  10.8 us
  transfers between devices with their start and end apart: 5, of which 2 were waited for; matrix products, arithmetic and copies ran while one was open for 27% of the time, Pallas kernels for 0%

commit v1 on v0

v1 whole, which is shorter than its diff:
```python
import functools
import math

import jax
import jax.numpy as jnp
from jax import lax
from jax.experimental import pallas as pl
from jax.experimental.pallas import tpu as pltpu
from jax.sharding import PartitionSpec as P

AXES = ("group", "span")
F32 = jnp.float32
BF16 = jnp.bfloat16
ROWS = (((0,), (0,)), ((), ()))
COLS = (((1,), (1,)), ((), ()))


def shifted(block, axis, distance):
    devices = range(lax.axis_size(axis))
    route = [(i - distance, i) for i in devices if i - distance in devices]
    return lax.ppermute(block, axis, route)


def dot(a, b, dims=(((1,), (0,)), ((), ()))):
    return lax.dot_general(a, b, dims, preferred_element_type=F32)


def summary_kernel(lin_scale, size, q, k, v, g, col, out):
    heads = q.shape[1] // size
    states, grads = [], []
    for j in range(heads):
        cut = slice(j * size, (j + 1) * size)
        run = col[0, :, j : j + 1]
        fading = jnp.exp(run[run.shape[0] - 1 :, :] - run)
        weighted = (v[:, cut].astype(F32) * fading).astype(BF16)
        scaled = (g[:, cut].astype(F32) * jnp.exp(run)).astype(BF16)
        states.append(dot(k[:, cut], weighted, ROWS))
        grads.append(lin_scale * dot(q[:, cut], scaled, ROWS))
    out[:size, :] = jnp.concatenate(states, axis=1).astype(BF16)
    out[size:, :] = jnp.concatenate(grads, axis=1).astype(BF16)


def near_kernel(
    lin_scale, soft_scale, size, q, k, v, g, pk, pv, col, row, count,
    out, dq, own_k, own_v, prev_k, prev_v,
):
    rows = q.shape[0]
    heads = q.shape[1] // size
    t = lax.broadcasted_iota(jnp.int32, (rows, rows), 0)
    s = lax.broadcasted_iota(jnp.int32, (rows, rows), 1)
    lower = t >= s
    times = count[...]
    outs, dqs, dkv, dvv = [], [], [], []
    for j in range(heads):
        cut = slice(j * size, (j + 1) * size)
        qh, gh = q[:, cut], g[:, cut]
        kh = jnp.concatenate([k[:, cut], pk[:, cut]], axis=0)
        vh = jnp.concatenate([v[:, cut], pv[:, cut]], axis=0)
        decay = jnp.where(
            lower, jnp.exp(jnp.minimum(col[0, :, j : j + 1] - row[0, j : j + 1, :], 0.0)), 0.0
        ) * lin_scale
        score = dot(qh, kh, COLS)
        grad = dot(gh, vh, COLS)
        logits = jnp.where(times > 0.0, score * soft_scale, -1e30)
        peak = jnp.max(logits, axis=1, keepdims=True)
        terms = jnp.exp(logits - peak) * times
        probs = terms / jnp.sum(terms, axis=1, keepdims=True)
        inner = jnp.sum(probs * grad, axis=1, keepdims=True)
        dlogit = probs * (grad - inner) * soft_scale
        mix = jnp.concatenate(
            [probs[:, :rows] + score[:, :rows] * decay, probs[:, rows:]], axis=1
        ).astype(BF16)
        dmix = jnp.concatenate(
            [dlogit[:, :rows] + grad[:, :rows] * decay, dlogit[:, rows:]], axis=1
        ).astype(BF16)
        outs.append(dot(mix, vh))
        dqs.append(dot(dmix, kh))
        dkv.append(dot(dmix, qh, ROWS))
        dvv.append(dot(mix, gh, ROWS))
    out[...] = jnp.concatenate(outs, axis=1)
    dq[...] = jnp.concatenate(dqs, axis=1)
    dk = jnp.concatenate(dkv, axis=1)
    dv = jnp.concatenate(dvv, axis=1)
    own_k[...] = dk[:rows]
    own_v[...] = dv[:rows]
    prev_k[...] = dk[rows:].astype(BF16)
    prev_v[...] = dv[rows:].astype(BF16)


def state_kernel(
    lin_scale, size, q, k, v, g, col, gathered, wf, wb, out, dq, own_k, own_v,
    layer, delta, grad_k, grad_v,
):
    heads = q.shape[1] // size
    count = gathered.shape[0]

    def one(f, carry):
        block = gathered[f].astype(F32)
        return (
            carry[0] + wf[pl.ds(f, 1), :] * block[:size],
            carry[1] + wb[pl.ds(f, 1), :] * block[size:],
        )

    zero = jnp.zeros((size, q.shape[1]), F32)
    state, later = lax.fori_loop(0, count, one, (zero, zero), unroll=8)
    state, later = state.astype(BF16), later.astype(BF16)
    outs, dqs, dks, dvs = [], [], [], []
    for j in range(heads):
        cut = slice(j * size, (j + 1) * size)
        run = col[0, :, j : j + 1]
        growth = lin_scale * jnp.exp(run)
        fading = jnp.exp(run[run.shape[0] - 1 :, :] - run)
        st, lt = state[:, cut], later[:, cut]
        outs.append(growth * dot(q[:, cut], st))
        dqs.append(growth * dot(g[:, cut], st, COLS))
        dks.append(fading * dot(v[:, cut], lt, COLS))
        dvs.append(fading * dot(k[:, cut], lt))
    layer[...] = (out[...] + jnp.concatenate(outs, axis=1)).astype(BF16)
    delta[...] = (dq[...] + jnp.concatenate(dqs, axis=1)).astype(BF16)
    grad_k[...] = (own_k[...] + jnp.concatenate(dks, axis=1)).astype(BF16)
    grad_v[...] = (own_v[...] + jnp.concatenate(dvs, axis=1)).astype(BF16)


def attention_parts(row_count, feat_width, head_count):
    size = feat_width // head_count
    pair = 128 // size
    steps = head_count // pair
    lanes = pair * size
    wide = pl.BlockSpec((row_count, lanes), lambda i: (0, i))
    col = pl.BlockSpec((1, row_count, pair), lambda i: (i, 0, 0))
    row = pl.BlockSpec((1, pair, row_count), lambda i: (i, 0, 0))
    return size, pair, steps, lanes, wide, col, row


def project(inputs, weight):
    return dot(inputs, weight).astype(BF16)


def shards(tokens, query_weight, key_weight, value_weight, log_decay, neighbour_blocks, cotangent):
    row_count, feat_width = tokens.shape
    head_count = log_decay.shape[0]
    size, pair, steps, lanes, wide, col_spec, row_spec = attention_parts(
        row_count, feat_width, head_count
    )
    lin_scale = 1.0 / (size * math.sqrt(row_count))
    soft_scale = 1.0 / math.sqrt(size)
    devices = lax.axis_size(AXES)
    position = lax.axis_index(AXES)
    shape = lambda dtype: jax.ShapeDtypeStruct((row_count, feat_width), dtype)

    prev_tokens = shifted(tokens, AXES, 1)
    running = jnp.cumsum(log_decay, axis=1)
    totals = lax.all_gather(running[:, -1], AXES)
    row = running.reshape(steps, pair, row_count)
    col = row.transpose(0, 2, 1)
    query = project(tokens, query_weight)
    key = project(tokens, key_weight)
    value = project(tokens, value_weight)

    summary = pl.pallas_call(
        functools.partial(summary_kernel, lin_scale, size),
        grid=(steps,),
        in_specs=[wide] * 4 + [col_spec],
        out_specs=pl.BlockSpec((2 * size, lanes), lambda i: (0, i)),
        out_shape=jax.ShapeDtypeStruct((2 * size, feat_width), BF16),
        cost_estimate=pl.CostEstimate(flops=10**8, bytes_accessed=10**6, transcendentals=0),
    )(query, key, value, cotangent, col)
    gathered = lax.all_gather(summary, AXES)

    prev_key = project(prev_tokens, key_weight)
    prev_value = project(prev_tokens, value_weight)
    own_times = jnp.sum(neighbour_blocks == position).astype(F32)
    prev_times = jnp.sum(neighbour_blocks == position - 1).astype(F32)
    times = jnp.where(jnp.arange(2 * row_count) < row_count, own_times, prev_times)[None, :]
    out, dq, own_k, own_v, prev_gk, prev_gv = pl.pallas_call(
        functools.partial(near_kernel, lin_scale, soft_scale, size),
        grid=(steps,),
        in_specs=[wide] * 6 + [col_spec, row_spec, pl.BlockSpec((1, 2 * row_count), lambda i: (0, 0))],
        out_specs=[wide] * 6,
        out_shape=[shape(F32)] * 4 + [shape(BF16)] * 2,
        cost_estimate=pl.CostEstimate(flops=10**10, bytes_accessed=10**7, transcendentals=10**6),
    )(query, key, value, cotangent, prev_key, prev_value, col, row, times)

    owed = dot(prev_gk, key_weight, COLS) + dot(prev_gv, value_weight, COLS)
    owed = shifted(owed.astype(BF16), AXES, -1)

    places = jnp.arange(devices)
    ahead = places[None, :] > places[:, None]
    between = ahead & (places[None, :] < position)
    between_later = (places[None, :] < places[:, None]) & (places[None, :] > position)
    weigh = lambda mask: jnp.exp(jnp.sum(jnp.where(mask[:, :, None], totals[None], 0.0), axis=1))
    earlier = jnp.where(places[:, None] < position, weigh(between), 0.0)
    after = jnp.where(places[:, None] > position, weigh(between_later), 0.0)
    earlier = jnp.repeat(earlier, size, axis=1)
    after = jnp.repeat(after, size, axis=1)
    weight_spec = pl.BlockSpec((devices, lanes), lambda i: (0, i))
    layer_out, query_delta, grad_k, grad_v = pl.pallas_call(
        functools.partial(state_kernel, lin_scale, size),
        grid=(steps,),
        in_specs=[wide] * 4
        + [col_spec, pl.BlockSpec((devices, 2 * size, lanes), lambda i: (0, 0, i))]
        + [weight_spec] * 2
        + [wide] * 4,
        out_specs=[wide] * 4,
        out_shape=[shape(BF16)] * 4,
        cost_estimate=pl.CostEstimate(flops=10**9, bytes_accessed=10**7, transcendentals=0),
    )(query, key, value, cotangent, col, gathered, earlier, after, out, dq, own_k, own_v)

    grad_norm = 1.0 / math.sqrt(row_count * devices)
    query_part = dot(tokens, query_delta, ROWS)
    both = jnp.concatenate([tokens, prev_tokens], axis=0)
    key_part = dot(both, jnp.concatenate([grad_k, prev_gk], axis=0), ROWS)
    value_part = dot(both, jnp.concatenate([grad_v, prev_gv], axis=0), ROWS)
    grads = reduce_grads(
        [(part * grad_norm).astype(BF16) for part in (query_part, key_part, value_part)]
    )
    tokens_back = dot(query_delta, query_weight, COLS)
    tokens_back = tokens_back + dot(grad_k, key_weight, COLS) + dot(grad_v, value_weight, COLS)
    tokens_back = tokens_back + owed.astype(F32)
    return (layer_out, tokens_back.astype(BF16), *grads)


def reduce_grads(parts):
    return lax.psum(tuple(parts), AXES)


def solution(mesh):
    return jax.shard_map(
        shards,
        mesh=mesh,
        in_specs=(
            P(AXES, None),
            P(),
            P(),
            P(),
            P(None, AXES),
            P(AXES, None),
            P(AXES, None),
        ),
        out_specs=(P(AXES, None), P(AXES, None), P(), P(), P()),
        check_vma=False,
    )
```

time: 530 us -> 296 us (0.56); the launches traced: 523 us -> 295 us
  waiting for transfers between devices: 256 us -> 165 us
  matrix products: 98.1 us -> 21.8 us
  other arithmetic: 48.6 us -> 1.87 us
  local copies, waits for them, and re-layouts: 55.8 us -> 14.1 us
  Pallas kernels: 0 us -> 28.1 us
    psum x1, waiting for transfers between devices: 254 us -> 139 us  [reduce_grads(): return lax.psum(tuple(parts), AXES)]
    dot_general x31 -> x13, matrix products: 93.5 us -> 21.8 us  [dot(): return lax.dot_general(a, b, dims, preferred_element_type=F32)]
    add x31 -> x0, other arithmetic: 33.1 us -> none  [join_carry(): jnp.exp(later[0])[:, None] * earlier[1] + later[1]]
    pallas_call x0 -> x3, Pallas kernels: none -> 28.1 us  [the longest x1 11.8 us: shards(): pl.pallas_call(functools.partial(near_kernel, lin_scale, soft_scale, size...]
    reshape x6 -> x3, local copies, waits for them, and re-layouts: 17.8 us -> 2.58 us  [the longest x1 1.03 us: shards(): row = running.reshape(steps, pair, row_count)]
    all_gather x2 -> x1, waiting for transfers between devices: 0.01 us -> 12.2 us  [shards(): gathered = lax.all_gather(summary, AXES)]
    convert_element_type x5 -> x0, other arithmetic: 11.3 us -> none  [the longest x2 10.8 us: shards(): (part_sum * grad_norm).astype(jnp.bfloat16)]
    ppermute x2, waiting for transfers between devices: 2.59 us -> 13.4 us  [shifted(): return lax.ppermute(block, axis, route)]
  transfers between devices with their start and end apart: 5 -> 4, of which waited for: 2 -> 3; matrix products, arithmetic and copies ran while one was open for 27% -> 4% of each run, Pallas kernels for 0% -> 4%
where the time goes in v1:
time: 296 us; the launch traced here: 295 us
  waiting for transfers between devices  165 us (56%)
  blocking collectives  41.9 us (14%)
  Pallas kernels  28.1 us (9%)
  matrix products  21.8 us (7%)
  between operations  15.5 us (5%)
  local copies, waits for them, and re-layouts  14.1 us (5%)
  starting transfers between devices  6.26 us (2%)
    psum x1, waiting for transfers between devices, reduce_grads(): return lax.psum(tuple(parts), AXES)  139 us
    unnamed x1, blocking collectives  41.9 us
    dot_general x13, matrix products, dot(): return lax.dot_general(a, b, dims, preferred_element_type=F32)  21.8 us
    ppermute x2, waiting for transfers between devices, shifted(): return lax.ppermute(block, axis, route)  13.4 us
    all_gather x1, waiting for transfers between devices, shards(): gathered = lax.all_gather(summary, AXES)  12.2 us
    pallas_call x1, Pallas kernels, shards(): pl.pallas_call(functools.partial(near_kernel, lin_scale, soft_scale, size...  11.8 us
    unnamed x36, local copies, waits for them, and re-layouts  10.2 us
    pallas_call x1, Pallas kernels, shards(): pl.pallas_call(functools.partial(state_kernel, lin_scale, size), grid=(st...  9.55 us
  transfers between devices with their start and end apart: 4, of which 3 were waited for; matrix products, arithmetic and copies ran while one was open for 4% of the time, Pallas kernels for 4%

profile of v1, /device:TPU:0, one launch (start us, length us, event | category | flops | bytes accessed | tf_op | source)
XLA Modules:
  0.0 294.6 jit_solution(12544105631309358797)
XLA Ops:
  7.2 0.0 copy-start
  7.2 0.0 copy-start.5
  7.2 0.0 all-gather.4.cloned.1.call-start
  7.2 0.0 copy-start.1
  7.2 3.0 %convolution_convert_fusion.4.q = bf16[128,1024]{1,0:T(8,128)(2,1)} fusion(bf16[128,1024]{1,0:T(8,128)(2,1)} %param.7, bf16[1024,1024]{1,0:T(8,128)(2,1)} %param.8), kind=kOutput, calls=%fused_computation.11 | convolution fusion | flops 268566528 | bytes 2621440 | tf_op jit(solution)/shard_map/dot_general | solution.py:25
  10.2 0.0 copy-done
  10.2 0.0 copy-done.5
  10.2 1.1 convolution_convert_fusion.3.k
  11.4 0.0 copy-done.1
  11.4 1.2 convolution_convert_fusion.2.v
  12.5 0.0 copy-done.13
  12.5 0.3 reduce_window_sum.11
  12.8 1.0 copy.16
  13.8 6.7 %shard_map.110 = bf16[128,1024]{1,0:T(8,128)(2,1)} custom-call(bf16[128,1024]{1,0:T(8,128)(2,1)} %convolution_convert_fusion.4.q, bf16[128,1024]{1,0:T(8,128)(2,1)} %convolution_convert_fusion.3.k, bf16[128,1024]{1,0:T(8,128)(2,1)} %convolution_convert_fusion.2.v, bf16[128,1024]{1,0:T(8,128)(2,1)} %g.5, f32[8,128,2]{2,1,0:T(8,128)} %bitcast.30), custom_call_target="tpu_custom_call" | custom-call | flops 100000000 | bytes 1000000 | tf_op jit(solution)/shard_map/pallas_call | solution.py:160
  20.6 0.0 all-gather.4.cloned.1.call-update
  20.6 0.0 all-reduce.4.cloned.1.call-start
  20.6 4.9 %collective-permute-start = (bf16[128,1024]{1,0:T(8,128)(2,1)S(1)}, bf16[128,1024]{1,0:T(8,128)(2,1)S(1)}, u32[]{:S(2)}, u32[]{:S(2)}) collective-permute-start(bf16[128,1024]{1,0:T(8,128)(2,1)S(1)} %copy-done.5), channel_id=1, source_target_pairs={{0,1},{1,2},{2,3},{3,4},{4,5},{5,6},{6,7},{7,8},{8,9},{9,10},{10,1... | collective-permute-start | bytes 786440 | tf_op jit(solution)/shard_map/ppermute | solution.py:21
  25.6 0.2 slice_reduce_fusion
  25.7 0.2 dynamic-update-slice
  26.0 41.9 %all-reduce = f32[512]{0:T(512)S(1)} all-reduce(f32[512]{0:T(512)S(1)} %dynamic-update-slice), channel_id=3, replica_groups=mesh['group'=4,'span'=8] {'group','span'}, use_global_device_ids=true, to_apply=%add | all-reduce | flops 512 | bytes 4096
  67.9 0.1 reshape.104
  68.0 0.1 copy.17
  68.1 0.2 select_reduce_fusion
  68.3 0.1 exponential_select_fusion.1
  68.4 0.1 exponential_select_fusion
  68.5 0.0 copy-done.14
  68.5 0.6 fusion.10
  69.1 0.1 broadcast_in_dim.79
  69.3 0.8 reshape.101.wf
  70.0 0.1 broadcast_in_dim.82
  70.2 0.8 reshape.102.wb
  70.9 0.0 copy-done.12
  72.3 0.0 copy-start.2
  72.3 0.6 compare_select_fusion.count
  72.8 0.7 constant_dynamic-update-slice_fusion.1
  73.5 0.0 collective-permute-done
  73.6 0.7 constant_dynamic-update-slice_fusion
  74.3 1.2 convolution_convert_fusion.1.pk
  75.4 0.0 copy-done.2
  75.4 1.1 convolution_convert_fusion.pv
  76.6 11.8 %shard_map.111 = (f32[128,1024]{1,0:T(8,128)}, f32[128,1024]{1,0:T(8,128)}, f32[128,1024]{1,0:T(8,128)}, f32[128,1024]{1,0:T(8,128)}, bf16[128,1024]{1,0:T(8,128)(2,1)}, /*index=5*/bf16[128,1024]{1,0:T(8,128)(2,1)}) custom-call(bf16[128,1024]{1,0:T(8,128)(2,1)} %convolution_convert_fusion.4.q, bf16[128,1024]{1,0:T(8,128)(2,1)} %convolution_convert_fusion.3.k, ...), custom_call_target="tpu_custom_call" | custom-call | flops 10000000000 | bytes 10000000 | tf_op jit(solution)/shard_map/pallas_call | solution.py:175
  88.4 12.2 %all-gather.4.cloned.1.call-done = bf16[4096,1024]{1,0:T(8,128)(2,1)} async-done(((bf16[128,1024]{1,0:T(8,128)(2,1)}), bf16[4096,1024]{1,0:T(8,128)(2,1)}) %all-gather.4.cloned.1.call-update) | async-done | bytes 8388624 | tf_op jit(solution)/shard_map/all_gather | solution.py:168
  100.6 9.6 %shard_map.112 = (bf16[128,1024]{1,0:T(8,128)(2,1)}, bf16[128,1024]{1,0:T(8,128)(2,1)}, bf16[128,1024]{1,0:T(8,128)(2,1)}, bf16[128,1024]{1,0:T(8,128)(2,1)}) custom-call(bf16[128,1024]{1,0:T(8,128)(2,1)} %convolution_convert_fusion.4.q, bf16[128,1024]{1,0:T(8,128)(2,1)} %convolution_convert_fusion.3.k, bf16[128,1024]{1,0:T(8,128)(2,1)} %convolution_convert_fusion.2.v, ...), custom_call_target="tpu_custom_call" | custom-call | flops 1000000000 | bytes 10000000 | tf_op jit(solution)/shard_map/pallas_call | solution.py:197
  110.2 0.0 copy-start.10
  110.2 0.0 copy-start.11
  110.2 3.1 %fusion = bf16[1024,1024]{0,1:T(8,128)(2,1)} fusion(bf16[128,1024]{1,0:T(8,128)(2,1)} %get-tuple-element.20, bf16[128,1024]{1,0:T(8,128)(2,1)S(1)} %copy-done.5), kind=kOutput, calls=%fused_computation.3 | convolution fusion | flops 270532608 | bytes 2621440 | tf_op jit(solution)/shard_map/dot_general | solution.py:25
  113.3 3.2 %multiply_convert_fusion.1 = bf16[1024,1024]{1,0:T(8,128)(2,1)} fusion(bf16[256,1024]{1,0:T(8,128)(2,1)} %constant_dynamic-update-slice_fusion, bf16[128,1024]{1,0:T(8,128)(2,1)S(1)} %copy-done.10, bf16[128,1024]{1,0:T(8,128)(2,1)S(1)} %copy-done.11), kind=kOutput, calls=%fused_computation.1 | convolution fusion | flops 540016640 | bytes 3145728 | tf_op jit(solution)/shard_map/dot_general | solution.py:25
  116.5 0.0 copy-done.9
  116.5 3.1 %multiply_convert_fusion = bf16[1024,1024]{1,0:T(8,128)(2,1)} fusion(bf16[256,1024]{1,0:T(8,128)(2,1)} %constant_dynamic-update-slice_fusion, bf16[128,1024]{1,0:T(8,128)(2,1)S(1)} %copy-done.8, bf16[128,1024]{1,0:T(8,128)(2,1)S(1)} %copy-done.9), kind=kOutput, calls=%fused_computation | convolution fusion | flops 540016640 | bytes 3145728 | tf_op jit(solution)/shard_map/dot_general | solution.py:25
  119.6 0.0 all-reduce.4.cloned.1.call-update
  119.6 0.0 copy-start.3
  119.6 0.8 fusion.15
  120.4 0.7 copy-done.3
  121.2 0.8 fusion.1
  122.0 1.3 collective-permute-start.1
  123.4 0.8 fusion.14
  124.2 0.8 convolution_add_fusion.2
  125.0 13.4 %collective-permute-done.1 = bf16[128,1024]{1,0:T(8,128)(2,1)S(1)} collective-permute-done((bf16[128,1024]{1,0:T(8,128)(2,1)S(1)}, bf16[128,1024]{1,0:T(8,128)(2,1)S(1)}, u32[]{:S(2)}, u32[]{:S(2)}) %collective-permute-start.1) | collective-permute-done | bytes 262176 | tf_op jit(solution)/shard_map/ppermute | solution.py:21
  138.4 1.6 add_convert_fusion
  140.0 139.3 %all-reduce.4.cloned.1.call-done = (bf16[1024,1024]{0,1:T(8,128)(2,1)}, bf16[1024,1024]{1,0:T(8,128)(2,1)}, bf16[1024,1024]{1,0:T(8,128)(2,1)}) async-done(((bf16[1024,1024]{0,1:T(8,128)(2,1)}, bf16[1024,1024]{1,0:T(8,128)(2,1)}, bf16[1024,1024]{1,0:T(8,128)(2,1)}), (bf16[1024,1024]{0,1:T(8,128)(2,1)}, bf16[1024,1024]{1,0:T(8,128)(2,1)}, bf16[1024,1024]{1,0:T(8,128)(2,1)})) %all-reduce.4.cloned.1.call-update) | async-done | bytes 6291472 | tf_op jit(solution)/shard_map/psum | solution.py:224
  279.3 3.9 %copy.18 = bf16[1024,1024]{1,0:T(8,128)(2,1)} copy(bf16[1024,1024]{0,1:T(8,128)(2,1)} %get-tuple-element.44) | data formatting | bytes 4194304
  283.2 3.2 %copy.24 = bf16[1024,1024]{1,0:T(8,128)(2,1)} copy(bf16[1024,1024]{1,0:T(8,128)(2,1)} %get-tuple-element.52) | data formatting | bytes 4194304
  286.4 0.0 copy-done.6
  286.4 1.3 copy.25
  (17 shorter events, 0.1 us)
Async XLA Ops:
  7.2 3.1 %copy-start = (bf16[1024,1024]{1,0:T(8,128)(2,1)S(1)}, bf16[1024,1024]{1,0:T(8,128)(2,1)}, u32[]{:S(2)}) copy-start(bf16[1024,1024]{1,0:T(8,128)(2,1)} %param.9) | copy-start | bytes 6291460
  7.2 3.0 %copy-start.5 = (bf16[128,1024]{1,0:T(8,128)(2,1)S(1)}, bf16[128,1024]{1,0:T(8,128)(2,1)}, u32[]{:S(2)}) copy-start(bf16[128,1024]{1,0:T(8,128)(2,1)} %param.7) | copy-start | bytes 786436
  7.2 93.4 %all-gather.4.cloned.1.call-start = ((), (), s32[]{:S(2)}) async-start(), calls=%async_computation | async-start | bytes 8650752 | tf_op jit(solution)/shard_map/all_gather | solution.py:168
  7.2 4.1 %copy-start.1 = (bf16[1024,1024]{1,0:T(8,128)(2,1)S(1)}, bf16[1024,1024]{1,0:T(8,128)(2,1)}, u32[]{:S(2)}) copy-start(bf16[1024,1024]{1,0:T(8,128)(2,1)} %param.10) | copy-start | bytes 6291460
  10.2 2.3 copy-start.13
  11.4 57.1 %copy-start.14 = (s32[1,4]{1,0:T(1,128)S(1)}, s32[1,4]{1,0:T(1,128)}, u32[]{:S(2)}) copy-start(s32[1,4]{1,0:T(1,128)} %param.12) | copy-start | bytes 52
  12.8 58.1 %copy-start.12 = (f32[16,128]{1,0:T(8,128)}, f32[16,128]{1,0:T(8,128)S(1)}, u32[]{:S(2)}) copy-start(f32[16,128]{1,0:T(8,128)S(1)} %reduce_window_sum.11) | copy-start | bytes 24580
  20.6 258.7 %all-reduce.4.cloned.1.call-start = ((), (), s32[]{:S(2)}) async-start(), calls=%async_computation.1 | async-start | bytes 12582912 | tf_op jit(solution)/shard_map/psum | solution.py:224
  20.6 52.9 %collective-permute-start = (bf16[128,1024]{1,0:T(8,128)(2,1)S(1)}, bf16[128,1024]{1,0:T(8,128)(2,1)S(1)}, u32[]{:S(2)}, u32[]{:S(2)}) collective-permute-start(bf16[128,1024]{1,0:T(8,128)(2,1)S(1)} %copy-done.5), channel_id=1, source_target_pairs={{0,1},{1,2},{2,3},{3,4},{4,5},{5,6},{6,7},{7,8},{8,9},{9,10},{10,1... | collective-permute-start | bytes 786440 | tf_op jit(solution)/shard_map/ppermute | solution.py:21
  72.3 3.2 %copy-start.2 = (bf16[1024,1024]{1,0:T(8,128)(2,1)S(1)}, bf16[1024,1024]{1,0:T(8,128)(2,1)}, u32[]{:S(2)}) copy-start(bf16[1024,1024]{1,0:T(8,128)(2,1)} %param.10) | copy-start | bytes 6291460
  110.2 3.1 %copy-start.10 = (bf16[128,1024]{1,0:T(8,128)(2,1)S(1)}, bf16[128,1024]{1,0:T(8,128)(2,1)}, u32[]{:S(2)}) copy-start(bf16[128,1024]{1,0:T(8,128)(2,1)} %get-tuple-element.23) | copy-start | bytes 786436
  110.2 3.1 %copy-start.11 = (bf16[128,1024]{1,0:T(8,128)(2,1)S(1)}, bf16[128,1024]{1,0:T(8,128)(2,1)}, u32[]{:S(2)}) copy-start(bf16[128,1024]{1,0:T(8,128)(2,1)} %get-tuple-element.21) | copy-start | bytes 786436
  113.3 3.2 %copy-start.8 = (bf16[128,1024]{1,0:T(8,128)(2,1)S(1)}, bf16[128,1024]{1,0:T(8,128)(2,1)}, u32[]{:S(2)}) copy-start(bf16[128,1024]{1,0:T(8,128)(2,1)} %get-tuple-element.24) | copy-start | bytes 786436
  113.3 3.2 %copy-start.9 = (bf16[128,1024]{1,0:T(8,128)(2,1)S(1)}, bf16[128,1024]{1,0:T(8,128)(2,1)}, u32[]{:S(2)}) copy-start(bf16[128,1024]{1,0:T(8,128)(2,1)} %get-tuple-element.22) | copy-start | bytes 786436
  119.6 1.6 copy-start.3
  121.2 2.2 copy-start.4
  121.2 2.2 copy-start.7
  122.0 16.4 %collective-permute-start.1 = (bf16[128,1024]{1,0:T(8,128)(2,1)S(1)}, bf16[128,1024]{1,0:T(8,128)(2,1)S(1)}, u32[]{:S(2)}, u32[]{:S(2)}) collective-permute-start(bf16[128,1024]{1,0:T(8,128)(2,1)S(1)} %fusion.1), channel_id=1, source_target_pairs={{1,0},{2,1},{3,2},{4,3},{5,4},{6,5},{7,6},{8,7},{9,8},{10,9},{11,1... | collective-permute-start | bytes 786440 | tf_op jit(solution)/shard_map/ppermute | solution.py:21
  283.2 3.2 %copy-start.6 = (bf16[1024,1024]{1,0:T(8,128)(2,1)S(1)}, bf16[1024,1024]{1,0:T(8,128)(2,1)}, u32[]{:S(2)}) copy-start(bf16[1024,1024]{1,0:T(8,128)(2,1)} %get-tuple-element.53) | copy-start | bytes 6291460
Sparse Core Ops, SparseCore 0:
  20.7 79.8 all-gather.3
  119.7 159.5 all-reduce.3

commit v2 on v1

--- a/solution.py
+++ b/solution.py
@@ -12,6 +12,7 @@
 F32 = jnp.float32
 BF16 = jnp.bfloat16
 ROWS = (((0,), (0,)), ((), ()))
+MESH = pl.DeviceIdType.MESH
 COLS = (((1,), (1,)), ((), ()))
 
 
@@ -88,22 +89,11 @@
 
 
 def state_kernel(
-    lin_scale, size, q, k, v, g, col, gathered, wf, wb, out, dq, own_k, own_v,
+    lin_scale, size, q, k, v, g, col, carry, out, dq, own_k, own_v,
     layer, delta, grad_k, grad_v,
 ):
     heads = q.shape[1] // size
-    count = gathered.shape[0]
-
-    def one(f, carry):
-        block = gathered[f].astype(F32)
-        return (
-            carry[0] + wf[pl.ds(f, 1), :] * block[:size],
-            carry[1] + wb[pl.ds(f, 1), :] * block[size:],
-        )
-
-    zero = jnp.zeros((size, q.shape[1]), F32)
-    state, later = lax.fori_loop(0, count, one, (zero, zero), unroll=8)
-    state, later = state.astype(BF16), later.astype(BF16)
+    state, later = carry[:size, :], carry[size:, :]
     outs, dqs, dks, dvs = [], [], [], []
     for j in range(heads):
         cut = slice(j * size, (j + 1) * size)
@@ -144,13 +134,13 @@
     )
     lin_scale = 1.0 / (size * math.sqrt(row_count))
     soft_scale = 1.0 / math.sqrt(size)
-    devices = lax.axis_size(AXES)
+    sizes = tuple(lax.axis_size(name) for name in AXES)
+    devices = sizes[0] * sizes[1]
     position = lax.axis_index(AXES)
     shape = lambda dtype: jax.ShapeDtypeStruct((row_count, feat_width), dtype)
 
     prev_tokens = shifted(tokens, AXES, 1)
     running = jnp.cumsum(log_decay, axis=1)
-    totals = lax.all_gather(running[:, -1], AXES)
     row = running.reshape(steps, pair, row_count)
     col = row.transpose(0, 2, 1)
     query = project(tokens, query_weight)
@@ -165,7 +155,8 @@
         out_shape=jax.ShapeDtypeStruct((2 * size, feat_width), BF16),
         cost_estimate=pl.CostEstimate(flops=10**8, bytes_accessed=10**6, transcendentals=0),
     )(query, key, value, cotangent, col)
-    gathered = lax.all_gather(summary, AXES)
+    total = jnp.broadcast_to(jnp.repeat(running[:, -1], size)[None, :], (8, feat_width))
+    carry = carried(summary, total, sizes)
 
     prev_key = project(prev_tokens, key_weight)
     prev_value = project(prev_tokens, value_weight)
@@ -184,27 +175,16 @@
     owed = dot(prev_gk, key_weight, COLS) + dot(prev_gv, value_weight, COLS)
     owed = shifted(owed.astype(BF16), AXES, -1)
 
-    places = jnp.arange(devices)
-    ahead = places[None, :] > places[:, None]
-    between = ahead & (places[None, :] < position)
-    between_later = (places[None, :] < places[:, None]) & (places[None, :] > position)
-    weigh = lambda mask: jnp.exp(jnp.sum(jnp.where(mask[:, :, None], totals[None], 0.0), axis=1))
-    earlier = jnp.where(places[:, None] < position, weigh(between), 0.0)
-    after = jnp.where(places[:, None] > position, weigh(between_later), 0.0)
-    earlier = jnp.repeat(earlier, size, axis=1)
-    after = jnp.repeat(after, size, axis=1)
-    weight_spec = pl.BlockSpec((devices, lanes), lambda i: (0, i))
     layer_out, query_delta, grad_k, grad_v = pl.pallas_call(
         functools.partial(state_kernel, lin_scale, size),
         grid=(steps,),
         in_specs=[wide] * 4
-        + [col_spec, pl.BlockSpec((devices, 2 * size, lanes), lambda i: (0, 0, i))]
-        + [weight_spec] * 2
+        + [col_spec, pl.BlockSpec((2 * size, lanes), lambda i: (0, i))]
         + [wide] * 4,
         out_specs=[wide] * 4,
         out_shape=[shape(BF16)] * 4,
         cost_estimate=pl.CostEstimate(flops=10**9, bytes_accessed=10**7, transcendentals=0),
-    )(query, key, value, cotangent, col, gathered, earlier, after, out, dq, own_k, own_v)
+    )(query, key, value, cotangent, col, carry, out, dq, own_k, own_v)
 
     grad_norm = 1.0 / math.sqrt(row_count * devices)
     query_part = dot(tokens, query_delta, ROWS)
@@ -212,7 +192,8 @@
     key_part = dot(both, jnp.concatenate([grad_k, prev_gk], axis=0), ROWS)
     value_part = dot(both, jnp.concatenate([grad_v, prev_gv], axis=0), ROWS)
     grads = reduce_grads(
-        [(part * grad_norm).astype(BF16) for part in (query_part, key_part, value_part)]
+        [(part * grad_norm).astype(BF16) for part in (query_part, key_part, value_part)],
+        sizes,
     )
     tokens_back = dot(query_delta, query_weight, COLS)
     tokens_back = tokens_back + dot(grad_k, key_weight, COLS) + dot(grad_v, value_weight, COLS)
@@ -220,8 +201,189 @@
     return (layer_out, tokens_back.astype(BF16), *grads)
 
 
-def reduce_grads(parts):
-    return lax.psum(tuple(parts), AXES)
+def bits_of(axis, size):
+    return [(axis, k) for k in range(size.bit_length() - 1)]
+
+
+def bit_of(bit):
+    return (lax.axis_index(bit[0]) // 2 ** bit[1]) % 2
+
+
+def partner_of(bit):
+    place = {name: lax.axis_index(name) for name in AXES}
+    place[bit[0]] = place[bit[0]] + (1 - 2 * bit_of(bit)) * 2 ** bit[1]
+    return place
+
+
+def greet(bits):
+    barrier = pltpu.get_barrier_semaphore()
+    for bit in bits:
+        pl.semaphore_signal(barrier, inc=1, device_id=partner_of(bit), device_id_type=MESH)
+    pl.semaphore_wait(barrier, len(bits))
+
+
+def carry_kernel(bits, size, x, total, out, sent, came, sums, sums_came, carry, sem, sum_sem):
+    greet(bits)
+    stages = len(bits)
+    width = x.shape[1]
+    tf = x[:size, :].astype(F32)
+    tb = x[size:, :].astype(F32)
+    carry[...] = jnp.zeros_like(carry)
+    log_all = total[...]
+    log_before = jnp.zeros_like(log_all)
+    log_after = jnp.zeros_like(log_all)
+    for i, bit in enumerate(bits):
+        mine = bit_of(bit)
+        if i:
+            sums[i] = log_all
+            sent[i, :size, :] = tf.astype(BF16)
+            sent[i, size:, :] = tb.astype(BF16)
+        copies = [
+            pltpu.make_async_remote_copy(
+                src_ref=sent.at[i] if i else x, dst_ref=came.at[i],
+                send_sem=sem.at[0, i], recv_sem=sem.at[1, i],
+                device_id=partner_of(bit), device_id_type=MESH,
+            ),
+            pltpu.make_async_remote_copy(
+                src_ref=sums.at[i] if i else total, dst_ref=sums_came.at[i],
+                send_sem=sum_sem.at[0, i], recv_sem=sum_sem.at[1, i],
+                device_id=partner_of(bit), device_id_type=MESH,
+            ),
+        ]
+        for copy in copies:
+            copy.start()
+        for copy in copies:
+            copy.wait()
+        log_other = sums_came[i]
+        f_other = came[i, :size, :].astype(F32)
+        b_other = came[i, size:, :].astype(F32)
+        second = jnp.full((1, width), mine) == 1
+        scale = jnp.exp(jnp.where(second, log_before, log_after)[:1])
+        carry[:size, :] += jnp.where(second, scale, 0.0) * f_other
+        carry[size:, :] += jnp.where(second, 0.0, scale) * b_other
+        log_before = log_before + jnp.where(second, log_other, 0.0)
+        log_after = log_after + jnp.where(second, 0.0, log_other)
+        if i + 1 < stages:
+            here, there = jnp.exp(log_all[:1]), jnp.exp(log_other[:1])
+            one = jnp.ones_like(here)
+            tf = jnp.where(second, one, there) * tf + jnp.where(second, here, one) * f_other
+            tb = jnp.where(second, there, one) * tb + jnp.where(second, one, here) * b_other
+            log_all = log_all + log_other
+    out[...] = carry[...].astype(BF16)
+
+
+def carried(summary, total, sizes):
+    bits = bits_of("span", sizes[1]) + bits_of("group", sizes[0])
+    rows, width = summary.shape
+    stages = len(bits)
+    vmem = pl.BlockSpec(memory_space=pltpu.VMEM)
+    return pl.pallas_call(
+        functools.partial(carry_kernel, bits, rows // 2),
+        in_specs=[vmem, vmem],
+        out_specs=vmem,
+        out_shape=jax.ShapeDtypeStruct((rows, width), BF16),
+        scratch_shapes=[
+            pltpu.VMEM((stages, rows, width), BF16),
+            pltpu.VMEM((stages, rows, width), BF16),
+            pltpu.VMEM((stages, 8, width), F32),
+            pltpu.VMEM((stages, 8, width), F32),
+            pltpu.VMEM((rows, width), F32),
+            pltpu.SemaphoreType.DMA((2, stages)),
+            pltpu.SemaphoreType.DMA((2, stages)),
+        ],
+        compiler_params=pltpu.CompilerParams(collective_id=0, has_side_effects=True),
+        cost_estimate=pl.CostEstimate(flops=10**9, bytes_accessed=10**8, transcendentals=0),
+    )(summary, total)
+
+
+def reduce_kernel(orders, *refs):
+    count = len(orders)
+    parts, outs = refs[:count], refs[count : 2 * count]
+    held, acc, sem = refs[2 * count :]
+    stages = len(orders[0])
+    whole = parts[0].shape[0]
+    greet(orders[0])
+    low = [[0] for _ in orders]
+
+    def halves(p, i):
+        half = whole >> (i + 1)
+        mine = bit_of(orders[p][i])
+        keep = low[p][i] + mine * half
+        give = low[p][i] + (1 - mine) * half
+        return half, keep, give
+
+    def copy(src, dst, p, i, slot):
+        return pltpu.make_async_remote_copy(
+            src_ref=src, dst_ref=dst, send_sem=sem.at[0, p, slot], recv_sem=sem.at[1, p, slot],
+            device_id=partner_of(orders[p][i]), device_id_type=MESH,
+        )
+
+    def scatter(p, i):
+        half, keep, give = halves(p, i)
+        source = parts[p] if i == 0 else acc.at[p]
+        place = whole - 2 * half
+        return copy(source.at[pl.ds(give, half)], held.at[p, pl.ds(place, half)], p, i, i)
+
+    def gather(p, i):
+        half, keep, _ = halves(p, i)
+        block = outs[p].at[pl.ds(keep, half)]
+        return copy(block, block, p, i, stages + i)
+
+    going = []
+    for p in range(count):
+        going.append(scatter(p, 0))
+        going[p].start()
+    for i in range(stages):
+        for p in range(count):
+            going[p].wait()
+            half, keep, _ = halves(p, i)
+            source = parts[p] if i == 0 else acc.at[p]
+            target = acc.at[p] if i + 1 < stages else outs[p]
+            place = whole - 2 * half
+            step = min(half, 8)
+
+            def add(c, _):
+                at = pl.ds(keep + c * step, step)
+                target[at] = source[at] + held[p, pl.ds(place + c * step, step)]
+                return 0
+
+            lax.fori_loop(0, half // step, add, 0)
+            low[p].append(keep)
+            going[p] = scatter(p, i + 1) if i + 1 < stages else gather(p, i)
+            going[p].start()
+    for i in reversed(range(stages)):
+        for p in range(count):
+            going[p].wait()
+            if i:
+                going[p] = gather(p, i - 1)
+                going[p].start()
+
+
+def reduce_grads(parts, sizes):
+    group, span = bits_of("group", sizes[0]), bits_of("span", sizes[1])
+    rest = group[1:] + span
+    turns = [rest[k:3] + rest[:k] + rest[3:] for k in range(3)]
+    orders = [group[:1] + turn for turn in turns]
+    rows, width = parts[0].shape
+    deep = (rows // 8, 8, width)
+    vmem = pl.BlockSpec(memory_space=pltpu.VMEM)
+    stages = len(orders[0])
+    outs = pl.pallas_call(
+        functools.partial(reduce_kernel, orders),
+        in_specs=[vmem] * 3,
+        out_specs=[vmem] * 3,
+        out_shape=[jax.ShapeDtypeStruct(deep, BF16)] * 3,
+        scratch_shapes=[
+            pltpu.VMEM((3, *deep), BF16),
+            pltpu.VMEM((3, *deep), BF16),
+            pltpu.SemaphoreType.DMA((2, 3, 2 * stages)),
+        ],
+        compiler_params=pltpu.CompilerParams(
+            collective_id=1, has_side_effects=True, vmem_limit_bytes=40 * 2**20
+        ),
+        cost_estimate=pl.CostEstimate(flops=10**9, bytes_accessed=10**8, transcendentals=0),
+    )(*[part.reshape(deep) for part in parts])
+    return [out.reshape(rows, width) for out in outs]
 
 
 def solution(mesh):

time: 296 us -> 206 us (0.70)
  waiting for transfers between devices: 165 us -> 0.01 us
  Pallas kernels: 28.1 us -> 148 us
  blocking collectives: 41.9 us -> 0 us
  between operations: 15.5 us -> 2.18 us
  local copies, waits for them, and re-layouts: 14.1 us -> 21.7 us
    psum x1 -> x0, waiting for transfers between devices: 139 us -> none  [reduce_grads(): return lax.psum(tuple(parts), AXES)]
    pallas_call x0 -> x2, Pallas kernels: none -> 123 us  [the longest x1 79.2 us: reduce_grads(): pl.pallas_call(functools.partial(reduce_kernel, orders), in_specs=[vmem]...]
    unnamed x1 -> x0, blocking collectives: 41.9 us -> none
    ppermute x2, waiting for transfers between devices: 13.4 us -> 0.01 us  [shifted(): return lax.ppermute(block, axis, route)]
    all_gather x1 -> x0, waiting for transfers between devices: 12.2 us -> none  [shards(): gathered = lax.all_gather(summary, AXES)]
    convert_element_type x0 -> x2, local copies, waits for them, and re-layouts: none -> 7.93 us  [shards(): (part * grad_norm).astype(BF16)]
    unnamed x36 -> x44, local copies, waits for them, and re-layouts: 10.2 us -> 11.7 us
  transfers between devices with their start and end apart: 4 -> 2, of which waited for: 3 -> 0; matrix products, arithmetic and copies ran while one was open for 4% -> 12% of each run, Pallas kernels for 4% -> 63%
where the time goes in v2:
time: 206 us; the launch traced here: 205 us
  Pallas kernels  148 us (72%)
  matrix products  24.1 us (12%)
  local copies, waits for them, and re-layouts  21.7 us (11%)
  starting transfers between devices  6.31 us (3%)
  other arithmetic  2.2 us (1%)
  between operations  2.18 us (1%)
    pallas_call x1, Pallas kernels, reduce_grads(): pl.pallas_call(functools.partial(reduce_kernel, orders), in_specs=[vmem]...  79.2 us
    pallas_call x1, Pallas kernels, carried(): pl.pallas_call(functools.partial(carry_kernel, bits, rows // 2), in_specs...  43.4 us
    dot_general x13, matrix products, dot(): return lax.dot_general(a, b, dims, preferred_element_type=F32)  24.1 us
    pallas_call x1, Pallas kernels, shards(): pl.pallas_call(functools.partial(near_kernel, lin_scale, soft_scale, size...  11.8 us
    unnamed x44, local copies, waits for them, and re-layouts  11.7 us
    convert_element_type x2, local copies, waits for them, and re-layouts, shards(): (part * grad_norm).astype(BF16)  7.93 us
    pallas_call x1, Pallas kernels, shards(): pl.pallas_call(functools.partial(state_kernel, lin_scale, size), grid=(st...  7.05 us
    pallas_call x1, Pallas kernels, shards(): pl.pallas_call(functools.partial(summary_kernel, lin_scale, size), grid=(...  6.73 us
  transfers between devices with their start and end apart: 2, of which 0 were waited for; matrix products, arithmetic and copies ran while one was open for 12% of the time, Pallas kernels for 63%

profile of v2, /device:TPU:0, one launch (start us, length us, event | category | flops | bytes accessed | tf_op | source)
XLA Modules:
  0.0 204.6 jit_solution(9864916593769446615)
XLA Ops:
  0.6 0.0 copy-start
  0.6 0.0 copy-start.7
  0.7 5.0 %collective-permute-start = (bf16[128,1024]{1,0:T(8,128)(2,1)}, bf16[128,1024]{1,0:T(8,128)(2,1)S(1)}, u32[]{:S(2)}, u32[]{:S(2)}) collective-permute-start(bf16[128,1024]{1,0:T(8,128)(2,1)} %param.7), channel_id=1, source_target_pairs={{0,1},{1,2},{2,3},{3,4},{4,5},{5,6},{6,7},{7,8},{8,9},{9,10},{10,1... | collective-permute-start | bytes 786440 | tf_op jit(solution)/shard_map/ppermute | solution.py:22
  5.7 1.0 reduce_window_sum.11
  6.7 0.2 slice_reduce_fusion
  6.9 0.1 broadcast_in_dim.19
  6.9 0.1 broadcast_in_dim.20
  7.0 3.0 %convolution_convert_fusion.4.q = bf16[128,1024]{1,0:T(8,128)(2,1)} fusion(bf16[128,1024]{1,0:T(8,128)(2,1)} %param.7, bf16[1024,1024]{1,0:T(8,128)(2,1)} %param.8), kind=kOutput, calls=%fused_computation.11 | convolution fusion | flops 268566528 | bytes 2621440 | tf_op jit(solution)/shard_map/dot_general | solution.py:26
  10.0 0.0 copy-done
  10.0 0.0 copy-done.7
  10.0 1.2 convolution_convert_fusion.3.k
  11.2 0.0 copy-done.4
  11.2 1.2 convolution_convert_fusion.2.v
  12.3 0.0 copy-done.18
  12.3 1.0 copy.17
  13.4 0.0 copy-done.19
  13.4 0.7 fusion.8
  14.1 6.7 %shard_map.110.x = bf16[128,1024]{1,0:T(8,128)(2,1)} custom-call(bf16[128,1024]{1,0:T(8,128)(2,1)} %convolution_convert_fusion.4.q, bf16[128,1024]{1,0:T(8,128)(2,1)} %convolution_convert_fusion.3.k, bf16[128,1024]{1,0:T(8,128)(2,1)} %convolution_convert_fusion.2.v, bf16[128,1024]{1,0:T(8,128)(2,1)} %g.5, f32[8,128,2]{2,1,0:T(8,128)} %bitcast.40), custom_call_target="tpu_custom_call" | custom-call | flops 100000000 | bytes 1000000 | tf_op jit(solution)/shard_map/pallas_call | solution.py:150
  20.8 0.6 broadcast_in_dim.21.total
  21.4 43.4 %shard_map.111.carry = bf16[128,1024]{1,0:T(8,128)(2,1)} custom-call(bf16[128,1024]{1,0:T(8,128)(2,1)} %shard_map.110.x, f32[8,1024]{1,0:T(8,128)} %broadcast_in_dim.21.total), custom_call_target="tpu_custom_call" | custom-call | flops 1000000000 | bytes 100000000 | tf_op jit(solution)/shard_map/pallas_call | solution.py:280
  66.2 0.5 compare_select_fusion.count
  66.7 0.7 constant_dynamic-update-slice_fusion.1
  67.4 0.0 collective-permute-done
  67.4 2.8 %convolution_convert_fusion.pv = bf16[128,1024]{1,0:T(8,128)(2,1)} fusion(bf16[128,1024]{1,0:T(8,128)(2,1)S(1)} %collective-permute-done, bf16[1024,1024]{1,0:T(8,128)(2,1)} %param.10), kind=kOutput, calls=%fused_computation.7 | convolution fusion | flops 268566528 | bytes 2621440 | tf_op jit(solution)/shard_map/dot_general | solution.py:26
  70.2 1.1 convolution_convert_fusion.1.pk
  71.3 11.8 %shard_map.112 = (f32[128,1024]{1,0:T(8,128)}, f32[128,1024]{1,0:T(8,128)}, f32[128,1024]{1,0:T(8,128)}, f32[128,1024]{1,0:T(8,128)}, bf16[128,1024]{1,0:T(8,128)(2,1)}, /*index=5*/bf16[128,1024]{1,0:T(8,128)(2,1)}) custom-call(bf16[128,1024]{1,0:T(8,128)(2,1)} %convolution_convert_fusion.4.q, bf16[128,1024]{1,0:T(8,128)(2,1)} %convolution_convert_fusion.3.k, ...), custom_call_target="tpu_custom_call" | custom-call | flops 10000000000 | bytes 10000000 | tf_op jit(solution)/shard_map/pallas_call | solution.py:166
  83.2 7.1 %shard_map.113 = (bf16[128,1024]{1,0:T(8,128)(2,1)}, bf16[128,1024]{1,0:T(8,128)(2,1)}, bf16[128,1024]{1,0:T(8,128)(2,1)}, bf16[128,1024]{1,0:T(8,128)(2,1)}) custom-call(bf16[128,1024]{1,0:T(8,128)(2,1)} %convolution_convert_fusion.4.q, bf16[128,1024]{1,0:T(8,128)(2,1)} %convolution_convert_fusion.3.k, bf16[128,1024]{1,0:T(8,128)(2,1)} %convolution_convert_fusion.2.v, ...), custom_call_target="tpu_custom_call" | custom-call | flops 1000000000 | bytes 10000000 | tf_op jit(solution)/shard_map/pallas_call | solution.py:178
  90.2 0.0 copy-start.8
  90.2 0.0 copy-start.14
  90.2 2.6 %fusion.12 = f32[128,1024]{1,0:T(8,128)S(1)} fusion(bf16[128,1024]{1,0:T(8,128)(2,1)} %get-tuple-element.23, bf16[1024,1024]{1,0:T(8,128)(2,1)} %param.8), kind=kOutput, calls=%fused_computation.30 | convolution fusion | flops 268435456 | bytes 2883584 | tf_op jit(solution)/shard_map/dot_general | solution.py:26
  92.8 0.0 copy-done.8
  92.8 2.1 %fusion.refs_0_ = bf16[128,8,1024]{2,1,0:T(8,128)(2,1)} fusion(bf16[128,1024]{1,0:T(8,128)(2,1)S(1)} %copy-done.8, bf16[128,1024]{1,0:T(8,128)(2,1)S(1)} %copy-done.7), kind=kOutput, calls=%fused_computation.3 | convolution fusion | flops 270532608 | bytes 2621440 | tf_op jit(solution)/shard_map/dot_general | solution.py:26
  94.9 0.0 copy-done.14
  94.9 0.8 fusion.13
  95.7 0.0 copy-start.16
  95.8 0.0 copy-start.10
  95.8 0.7 copy-done.5
  96.5 0.0 copy-done.9
  96.5 0.8 fusion.1
  97.3 1.3 collective-permute-start.1
  98.6 0.0 copy-done.16
  98.7 0.0 copy-start.17
  98.7 0.8 copy-done.17
  99.5 0.0 copy-done.10
  99.5 2.1 %multiply_convert_fusion = bf16[1024,1024]{0,1:T(8,128)(2,1)} fusion(bf16[256,1024]{1,0:T(8,128)(2,1)S(1)} %constant_dynamic-update-slice_fusion, bf16[128,1024]{1,0:T(8,128)(2,1)S(1)} %copy-done.9, bf16[128,1024]{1,0:T(8,128)(2,1)S(1)} %copy-done.10), kind=kOutput, calls=%fused_computation | convolution fusion | flops 540016640 | bytes 3145728 | tf_op jit(solution)/shard_map/dot_general | solution.py:26
  101.6 4.0 %copy.21 = bf16[1024,1024]{1,0:T(8,128)(2,1)} copy(bf16[1024,1024]{0,1:T(8,128)(2,1)} %multiply_convert_fusion) | data formatting | bytes 4194304 | tf_op jit(solution)/shard_map/convert_element_type | solution.py:195
  105.6 0.0 copy-done.12
  105.6 0.0 copy-done.15
  105.6 3.1 %multiply_convert_fusion.1 = bf16[1024,1024]{0,1:T(8,128)(2,1)} fusion(bf16[256,1024]{1,0:T(8,128)(2,1)} %copy-done.17, bf16[128,1024]{1,0:T(8,128)(2,1)S(1)} %copy-done.15, bf16[128,1024]{1,0:T(8,128)(2,1)S(1)} %copy-done.12), kind=kOutput, calls=%fused_computation.1 | convolution fusion | flops 540016640 | bytes 3145728 | tf_op jit(solution)/shard_map/dot_general | solution.py:26
  108.7 3.9 %copy.19 = bf16[1024,1024]{1,0:T(8,128)(2,1)} copy(bf16[1024,1024]{0,1:T(8,128)(2,1)} %multiply_convert_fusion.1) | data formatting | bytes 4194304 | tf_op jit(solution)/shard_map/convert_element_type | solution.py:195
  112.6 1.6 copy-done.1
  114.2 1.6 copy-done.2
  115.8 1.6 copy-done.3
  117.4 79.2 %shard_map.114 = (bf16[128,8,1024]{2,1,0:T(8,128)(2,1)S(1)}, bf16[128,8,1024]{2,1,0:T(8,128)(2,1)S(1)}, bf16[128,8,1024]{2,1,0:T(8,128)(2,1)S(1)}) custom-call(bf16[128,8,1024]{2,1,0:T(8,128)(2,1)S(1)} %copy-done.1, bf16[128,8,1024]{2,1,0:T(8,128)(2,1)S(1)} %bitcast.36, bf16[128,8,1024]{2,1,0:T(8,128)(2,1)S(1)} %bitcast.35), custom_call_target="tpu_custom_call" | custom-call | flops 1000000000 | bytes 100000000 | tf_op jit(solution)/shard_map/pallas_call | solution.py:371
  196.6 0.0 copy-start.6
  196.6 0.0 copy-start.11
  196.6 0.0 copy-done.13
  196.6 0.8 convolution_add_fusion.2
  197.4 0.0 collective-permute-done.1
  197.5 0.7 copy-done.6
  198.2 2.5 %add_convert_fusion = bf16[128,1024]{1,0:T(8,128)(2,1)} fusion(bf16[128,1024]{1,0:T(8,128)(2,1)} %collective-permute-done.1, f32[128,1024]{1,0:T(8,128)S(1)} %convolution_add_fusion.2, bf16[128,1024]{1,0:T(8,128)(2,1)S(1)} %copy-done.11, bf16[1024,1024]{1,0:T(8,128)(2,1)S(1)} %copy-done.6), kind=kOutput, calls=%fused_computation.19 | convolution fusion | flops 268959744 | bytes 3407872 | tf_op jit(solution)/shard_map/dot_general | solution.py:26
  200.7 1.3 copy.28
  202.0 1.3 copy.29
  203.3 1.3 copy.30
  (13 shorter events, 0.0 us)
Async XLA Ops:
  0.6 9.4 %copy-start = (bf16[1024,1024]{1,0:T(8,128)(2,1)S(1)}, bf16[1024,1024]{1,0:T(8,128)(2,1)}, u32[]{:S(2)}) copy-start(bf16[1024,1024]{1,0:T(8,128)(2,1)} %param.9) | copy-start | bytes 6291460
  0.6 9.3 %copy-start.7 = (bf16[128,1024]{1,0:T(8,128)(2,1)S(1)}, bf16[128,1024]{1,0:T(8,128)(2,1)}, u32[]{:S(2)}) copy-start(bf16[128,1024]{1,0:T(8,128)(2,1)} %param.7) | copy-start | bytes 786436
  0.7 66.8 %collective-permute-start = (bf16[128,1024]{1,0:T(8,128)(2,1)}, bf16[128,1024]{1,0:T(8,128)(2,1)S(1)}, u32[]{:S(2)}, u32[]{:S(2)}) collective-permute-start(bf16[128,1024]{1,0:T(8,128)(2,1)} %param.7), channel_id=1, source_target_pairs={{0,1},{1,2},{2,3},{3,4},{4,5},{5,6},{6,7},{7,8},{8,9},{9,10},{10,1... | collective-permute-start | bytes 786440 | tf_op jit(solution)/shard_map/ppermute | solution.py:22
  6.7 5.7 %copy-start.18 = (f32[16,128]{1,0:T(8,128)}, f32[16,128]{1,0:T(8,128)S(1)}, u32[]{:S(2)}) copy-start(f32[16,128]{1,0:T(8,128)S(1)} %reduce_window_sum.11) | copy-start | bytes 24580
  7.0 4.2 %copy-start.4 = (bf16[1024,1024]{1,0:T(8,128)(2,1)S(1)}, bf16[1024,1024]{1,0:T(8,128)(2,1)}, u32[]{:S(2)}) copy-start(bf16[1024,1024]{1,0:T(8,128)(2,1)} %param.10) | copy-start | bytes 6291460
  11.2 2.2 %copy-start.19 = (s32[1,4]{1,0:T(1,128)S(1)}, s32[1,4]{1,0:T(1,128)}, u32[]{:S(2)}) copy-start(s32[1,4]{1,0:T(1,128)} %param.12) | copy-start | bytes 52
  90.2 2.6 %copy-start.8 = (bf16[128,1024]{1,0:T(8,128)(2,1)S(1)}, bf16[128,1024]{1,0:T(8,128)(2,1)}, u32[]{:S(2)}) copy-start(bf16[128,1024]{1,0:T(8,128)(2,1)} %get-tuple-element.23) | copy-start | bytes 786436
  90.2 4.7 %copy-start.14 = (bf16[128,1024]{1,0:T(8,128)(2,1)S(1)}, bf16[128,1024]{1,0:T(8,128)(2,1)}, u32[]{:S(2)}) copy-start(bf16[128,1024]{1,0:T(8,128)(2,1)} %get-tuple-element.26) | copy-start | bytes 786436
  94.9 1.6 copy-start.5
  94.9 1.6 copy-start.9
  95.7 2.9 %copy-start.16 = (bf16[256,1024]{1,0:T(8,128)(2,1)S(1)}, bf16[256,1024]{1,0:T(8,128)(2,1)}, u32[]{:S(2)}) copy-start(bf16[256,1024]{1,0:T(8,128)(2,1)} %constant_dynamic-update-slice_fusion.1) | copy-start | bytes 1572868
  95.8 3.7 %copy-start.10 = (bf16[128,1024]{1,0:T(8,128)(2,1)S(1)}, bf16[128,1024]{1,0:T(8,128)(2,1)}, u32[]{:S(2)}) copy-start(bf16[128,1024]{1,0:T(8,128)(2,1)} %get-tuple-element.25) | copy-start | bytes 786436
  97.3 100.1 %collective-permute-start.1 = (bf16[128,1024]{1,0:T(8,128)(2,1)S(1)}, bf16[128,1024]{1,0:T(8,128)(2,1)}, u32[]{:S(2)}, u32[]{:S(2)}) collective-permute-start(bf16[128,1024]{1,0:T(8,128)(2,1)S(1)} %fusion.1), channel_id=1, source_target_pairs={{1,0},{2,1},{3,2},{4,3},{5,4},{6,5},{7,6},{8,7},{9,8},{10,9},{11,1... | collective-permute-start | bytes 786440 | tf_op jit(solution)/shard_map/ppermute | solution.py:22
  98.7 0.8 copy-start.17
  101.6 4.0 %copy-start.12 = (bf16[128,1024]{1,0:T(8,128)(2,1)S(1)}, bf16[128,1024]{1,0:T(8,128)(2,1)}, u32[]{:S(2)}) copy-start(bf16[128,1024]{1,0:T(8,128)(2,1)} %get-tuple-element.24) | copy-start | bytes 786436
  101.6 4.0 %copy-start.15 = (bf16[128,1024]{1,0:T(8,128)(2,1)S(1)}, bf16[128,1024]{1,0:T(8,128)(2,1)}, u32[]{:S(2)}) copy-start(bf16[128,1024]{1,0:T(8,128)(2,1)} %get-tuple-element.26) | copy-start | bytes 786436
  112.6 1.6 copy-start.1
  114.2 1.6 copy-start.2
  115.8 1.6 copy-start.3
  117.4 79.2 %copy-start.13 = (bf16[128,1024]{1,0:T(8,128)(2,1)S(1)}, bf16[128,1024]{1,0:T(8,128)(2,1)}, u32[]{:S(2)}) copy-start(bf16[128,1024]{1,0:T(8,128)(2,1)} %get-tuple-element.24) | copy-start | bytes 786436
  196.6 1.6 copy-start.6
  196.6 1.6 copy-start.11

commit v3 on v2

--- a/solution.py
+++ b/solution.py
@@ -41,16 +41,12 @@
     out[size:, :] = jnp.concatenate(grads, axis=1).astype(BF16)
 
 
-def near_kernel(
-    lin_scale, soft_scale, size, q, k, v, g, pk, pv, col, row, count,
-    out, dq, own_k, own_v, prev_k, prev_v,
-):
+def near_pair(lin_scale, soft_scale, size, q, k, v, g, pk, pv, col, row, times):
     rows = q.shape[0]
     heads = q.shape[1] // size
     t = lax.broadcasted_iota(jnp.int32, (rows, rows), 0)
     s = lax.broadcasted_iota(jnp.int32, (rows, rows), 1)
     lower = t >= s
-    times = count[...]
     outs, dqs, dkv, dvv = [], [], [], []
     for j in range(heads):
         cut = slice(j * size, (j + 1) * size)
@@ -58,7 +54,7 @@
         kh = jnp.concatenate([k[:, cut], pk[:, cut]], axis=0)
         vh = jnp.concatenate([v[:, cut], pv[:, cut]], axis=0)
         decay = jnp.where(
-            lower, jnp.exp(jnp.minimum(col[0, :, j : j + 1] - row[0, j : j + 1, :], 0.0)), 0.0
+            lower, jnp.exp(jnp.minimum(col[:, j : j + 1] - row[j : j + 1, :], 0.0)), 0.0
         ) * lin_scale
         score = dot(qh, kh, COLS)
         grad = dot(gh, vh, COLS)
@@ -78,14 +74,16 @@
         dqs.append(dot(dmix, kh))
         dkv.append(dot(dmix, qh, ROWS))
         dvv.append(dot(mix, gh, ROWS))
-    out[...] = jnp.concatenate(outs, axis=1)
-    dq[...] = jnp.concatenate(dqs, axis=1)
     dk = jnp.concatenate(dkv, axis=1)
     dv = jnp.concatenate(dvv, axis=1)
-    own_k[...] = dk[:rows]
-    own_v[...] = dv[:rows]
-    prev_k[...] = dk[rows:].astype(BF16)
-    prev_v[...] = dv[rows:].astype(BF16)
+    return (
+        jnp.concatenate(outs, axis=1),
+        jnp.concatenate(dqs, axis=1),
+        dk[:rows],
+        dv[:rows],
+        dk[rows:].astype(BF16),
+        dv[rows:].astype(BF16),
+    )
 
 
 def state_kernel(
@@ -156,21 +154,15 @@
         cost_estimate=pl.CostEstimate(flops=10**8, bytes_accessed=10**6, transcendentals=0),
     )(query, key, value, cotangent, col)
     total = jnp.broadcast_to(jnp.repeat(running[:, -1], size)[None, :], (8, feat_width))
-    carry = carried(summary, total, sizes)
 
     prev_key = project(prev_tokens, key_weight)
     prev_value = project(prev_tokens, value_weight)
     own_times = jnp.sum(neighbour_blocks == position).astype(F32)
     prev_times = jnp.sum(neighbour_blocks == position - 1).astype(F32)
     times = jnp.where(jnp.arange(2 * row_count) < row_count, own_times, prev_times)[None, :]
-    out, dq, own_k, own_v, prev_gk, prev_gv = pl.pallas_call(
-        functools.partial(near_kernel, lin_scale, soft_scale, size),
-        grid=(steps,),
-        in_specs=[wide] * 6 + [col_spec, row_spec, pl.BlockSpec((1, 2 * row_count), lambda i: (0, 0))],
-        out_specs=[wide] * 6,
-        out_shape=[shape(F32)] * 4 + [shape(BF16)] * 2,
-        cost_estimate=pl.CostEstimate(flops=10**10, bytes_accessed=10**7, transcendentals=10**6),
-    )(query, key, value, cotangent, prev_key, prev_value, col, row, times)
+    near = functools.partial(near_pair, lin_scale, soft_scale, size)
+    operands = (query, key, value, cotangent, prev_key, prev_value, col, row, times)
+    carry, out, dq, own_k, own_v, prev_gk, prev_gv = carried(near, summary, total, operands, sizes)
 
     owed = dot(prev_gk, key_weight, COLS) + dot(prev_gv, value_weight, COLS)
     owed = shifted(owed.astype(BF16), AXES, -1)
@@ -187,12 +179,9 @@
     )(query, key, value, cotangent, col, carry, out, dq, own_k, own_v)
 
     grad_norm = 1.0 / math.sqrt(row_count * devices)
-    query_part = dot(tokens, query_delta, ROWS)
-    both = jnp.concatenate([tokens, prev_tokens], axis=0)
-    key_part = dot(both, jnp.concatenate([grad_k, prev_gk], axis=0), ROWS)
-    value_part = dot(both, jnp.concatenate([grad_v, prev_gv], axis=0), ROWS)
     grads = reduce_grads(
-        [(part * grad_norm).astype(BF16) for part in (query_part, key_part, value_part)],
+        grad_norm,
+        (tokens, prev_tokens, query_delta, grad_k, grad_v, prev_gk, prev_gv),
         sizes,
     )
     tokens_back = dot(query_delta, query_weight, COLS)
@@ -222,7 +211,20 @@
     pl.semaphore_wait(barrier, len(bits))
 
 
-def carry_kernel(bits, size, x, total, out, sent, came, sums, sums_came, carry, sem, sum_sem):
+def carry_kernel(bits, near, size, x, total, *refs):
+    ins, col, row, count = refs[:6], refs[6], refs[7], refs[8]
+    out, results = refs[9], refs[10:16]
+    sent, came, sums, sums_came, carry, sem, sum_sem = refs[16:]
+    steps, _, pair = col.shape
+    lanes = pair * size
+
+    def near_step(i, _):
+        cut = pl.ds(pl.multiple_of(i * lanes, lanes), lanes)
+        values = near(*(ref[:, cut] for ref in ins), col[i], row[i], count[...])
+        for ref, value in zip(results, values):
+            ref[:, cut] = value
+        return 0
+
     greet(bits)
     stages = len(bits)
     width = x.shape[1]
@@ -252,6 +254,7 @@
         ]
         for copy in copies:
             copy.start()
+        lax.fori_loop(steps * i // stages, steps * (i + 1) // stages, near_step, 0)
         for copy in copies:
             copy.wait()
         log_other = sums_came[i]
@@ -272,16 +275,18 @@
     out[...] = carry[...].astype(BF16)
 
 
-def carried(summary, total, sizes):
+def carried(near, summary, total, operands, sizes):
     bits = bits_of("span", sizes[1]) + bits_of("group", sizes[0])
     rows, width = summary.shape
     stages = len(bits)
     vmem = pl.BlockSpec(memory_space=pltpu.VMEM)
     return pl.pallas_call(
-        functools.partial(carry_kernel, bits, rows // 2),
-        in_specs=[vmem, vmem],
-        out_specs=vmem,
-        out_shape=jax.ShapeDtypeStruct((rows, width), BF16),
+        functools.partial(carry_kernel, bits, near, rows // 2),
+        in_specs=[vmem] * (2 + len(operands)),
+        out_specs=[vmem] * 7,
+        out_shape=[jax.ShapeDtypeStruct((rows, width), BF16)]
+        + [jax.ShapeDtypeStruct(operands[0].shape, F32)] * 4
+        + [jax.ShapeDtypeStruct(operands[0].shape, BF16)] * 2,
         scratch_shapes=[
             pltpu.VMEM((stages, rows, width), BF16),
             pltpu.VMEM((stages, rows, width), BF16),
@@ -293,16 +298,34 @@
         ],
         compiler_params=pltpu.CompilerParams(collective_id=0, has_side_effects=True),
         cost_estimate=pl.CostEstimate(flops=10**9, bytes_accessed=10**8, transcendentals=0),
-    )(summary, total)
-
-
-def reduce_kernel(orders, *refs):
+    )(summary, total, *operands)
+
+
+def reduce_kernel(orders, norm, tokens, prev, dq, dk, dv, pk, pv, *refs):
     count = len(orders)
-    parts, outs = refs[:count], refs[count : 2 * count]
-    held, acc, sem = refs[2 * count :]
+    outs = refs[:count]
+    made, held, acc, sem = refs[count:]
+    parts = [made.at[p] for p in range(count)]
+    deltas = ((dq, None), (dk, pk), (dv, pv))
     stages = len(orders[0])
-    whole = parts[0].shape[0]
+    whole = outs[0].shape[0]
     greet(orders[0])
+
+    def make(p, start):
+        own, other = deltas[p]
+        right = own[...] if other is None else jnp.concatenate([own[...], other[...]], axis=0)
+
+        def one(c, _):
+            cut = pl.ds(pl.multiple_of(start * 8 + c * 128, 128), 128)
+            left = tokens[:, cut]
+            if other is not None:
+                left = jnp.concatenate([left, prev[:, cut]], axis=0)
+            block = dot(left, right, ROWS) * norm
+            made[p, pl.ds(start + c * 16, 16)] = block.reshape(16, 8, -1).astype(BF16)
+            return 0
+
+        lax.fori_loop(0, whole // 32, one, 0)
+
     low = [[0] for _ in orders]
 
     def halves(p, i):
@@ -331,8 +354,11 @@
 
     going = []
     for p in range(count):
+        make(p, halves(p, 0)[2])
         going.append(scatter(p, 0))
         going[p].start()
+    for p in range(count):
+        make(p, halves(p, 0)[1])
     for i in range(stages):
         for p in range(count):
             going[p].wait()
@@ -359,21 +385,22 @@
                 going[p].start()
 
 
-def reduce_grads(parts, sizes):
+def reduce_grads(norm, operands, sizes):
     group, span = bits_of("group", sizes[0]), bits_of("span", sizes[1])
     rest = group[1:] + span
     turns = [rest[k:3] + rest[:k] + rest[3:] for k in range(3)]
     orders = [group[:1] + turn for turn in turns]
-    rows, width = parts[0].shape
+    rows = width = operands[0].shape[1]
     deep = (rows // 8, 8, width)
     vmem = pl.BlockSpec(memory_space=pltpu.VMEM)
     stages = len(orders[0])
     outs = pl.pallas_call(
-        functools.partial(reduce_kernel, orders),
-        in_specs=[vmem] * 3,
+        functools.partial(reduce_kernel, orders, norm),
+        in_specs=[vmem] * len(operands),
         out_specs=[vmem] * 3,
         out_shape=[jax.ShapeDtypeStruct(deep, BF16)] * 3,
         scratch_shapes=[
+            pltpu.VMEM((3, *deep), BF16),
             pltpu.VMEM((3, *deep), BF16),
             pltpu.VMEM((3, *deep), BF16),
             pltpu.SemaphoreType.DMA((2, 3, 2 * stages)),
@@ -382,7 +409,7 @@
             collective_id=1, has_side_effects=True, vmem_limit_bytes=40 * 2**20
         ),
         cost_estimate=pl.CostEstimate(flops=10**9, bytes_accessed=10**8, transcendentals=0),
-    )(*[part.reshape(deep) for part in parts])
+    )(*operands)
     return [out.reshape(rows, width) for out in outs]
 
 

time: 206 us -> 173 us (0.84)
  local copies, waits for them, and re-layouts: 21.7 us -> 6.77 us
  matrix products: 24.1 us -> 15.8 us
  Pallas kernels: 148 us -> 140 us
    pallas_call x3 -> x2, Pallas kernels: 134 us -> 126 us  [the longest x1 80.8 us: reduce_grads(): pl.pallas_call(functools.partial(reduce_kernel, orders, norm), in_specs=[...]
    dot_general x13 -> x10, matrix products: 24.1 us -> 15.8 us  [dot(): return lax.dot_general(a, b, dims, preferred_element_type=F32)]
    convert_element_type x2 -> x0, local copies, waits for them, and re-layouts: 7.93 us -> none  [shards(): (part * grad_norm).astype(BF16)]
    unnamed x44 -> x27, local copies, waits for them, and re-layouts: 11.7 us -> 4.81 us
  transfers between devices with their start and end apart: 2 -> 2, of which waited for: 0 -> 0; matrix products, arithmetic and copies ran while one was open for 12% -> 5% of each run, Pallas kernels for 63% -> 51%
where the time goes in v3:
time: 173 us; the launch traced here: 172 us
  Pallas kernels  140 us (81%)
  matrix products  15.8 us (9%)
  local copies, waits for them, and re-layouts  6.77 us (4%)
  starting transfers between devices  6.49 us (4%)
  between operations  2.14 us (1%)
    pallas_call x1, Pallas kernels, reduce_grads(): pl.pallas_call(functools.partial(reduce_kernel, orders, norm), in_specs=[...  80.8 us
    pallas_call x1, Pallas kernels, carried(): pl.pallas_call(functools.partial(carry_kernel, bits, near, rows // 2), in...  45.1 us
    dot_general x10, matrix products, dot(): return lax.dot_general(a, b, dims, preferred_element_type=F32)  15.8 us
    pallas_call x1, Pallas kernels, shards(): pl.pallas_call(functools.partial(state_kernel, lin_scale, size), grid=(st...  7.03 us
    pallas_call x1, Pallas kernels, shards(): pl.pallas_call(functools.partial(summary_kernel, lin_scale, size), grid=(...  6.73 us
    ppermute x2, starting transfers between devices, shifted(): return lax.ppermute(block, axis, route)  6.49 us
    unnamed x27, local copies, waits for them, and re-layouts  4.81 us
  transfers between devices with their start and end apart: 2, of which 0 were waited for; matrix products, arithmetic and copies ran while one was open for 5% of the time, Pallas kernels for 51%

profile of v3, /device:TPU:0, one launch (start us, length us, event | category | flops | bytes accessed | tf_op | source)
XLA Modules:
  0.0 172.3 jit_solution(7855942138986329229)
XLA Ops:
  0.6 0.0 copy-start
  0.6 0.0 copy-start.1
  0.7 5.0 %collective-permute-start = (bf16[128,1024]{1,0:T(8,128)(2,1)}, bf16[128,1024]{1,0:T(8,128)(2,1)S(1)}, u32[]{:S(2)}, u32[]{:S(2)}) collective-permute-start(bf16[128,1024]{1,0:T(8,128)(2,1)} %tokens.1), channel_id=1, source_target_pairs={{0,1},{1,2},{2,3},{3,4},{4,5},{5,6},{6,7},{7,8},{8,9},{9,10},{10,1... | collective-permute-start | bytes 786440 | tf_op jit(solution)/shard_map/ppermute | solution.py:22
  5.7 0.0 copy-start.7
  5.7 3.0 %convolution_convert_fusion.4.q.refs_0_ = bf16[128,1024]{1,0:T(8,128)(2,1)} fusion(bf16[128,1024]{1,0:T(8,128)(2,1)} %tokens.1, bf16[1024,1024]{1,0:T(8,128)(2,1)} %param.8), kind=kOutput, calls=%fused_computation.7 | convolution fusion | flops 268566528 | bytes 2621440 | tf_op jit(solution)/shard_map/dot_general | solution.py:26
  8.7 0.0 copy-done
  8.7 0.0 copy-done.1
  8.7 0.0 copy-start.11
  8.7 0.0 copy-start.10
  8.7 1.2 convolution_convert_fusion.3.k.refs_1_
  9.8 0.0 copy-done.7
  9.8 1.2 convolution_convert_fusion.2.v.refs_2_
  11.0 0.0 copy-done.11
  11.0 0.6 fusion.1
  12.9 0.0 copy-done.10
  12.9 0.3 reduce_window_sum.11
  13.2 0.0 copy-start.9
  13.2 0.2 slice_reduce_fusion
  13.4 0.1 broadcast_in_dim.19
  13.5 0.1 broadcast_in_dim.20
  13.6 1.0 copy.13
  14.6 6.7 %shard_map.110.x = bf16[128,1024]{1,0:T(8,128)(2,1)} custom-call(bf16[128,1024]{1,0:T(8,128)(2,1)} %convolution_convert_fusion.4.q.refs_0_, bf16[128,1024]{1,0:T(8,128)(2,1)} %convolution_convert_fusion.3.k.refs_1_, bf16[128,1024]{1,0:T(8,128)(2,1)} %convolution_convert_fusion.2.v.refs_2_, bf16[128,1024]{1,0:T(8,128)(2,1)} %g.3, f32[8,128,2]{2,1,0:T(8,128)} %bitcast.28), custom_call_target="tpu_custom_call" | custom-call | flops 100000000 | bytes 1000000 | tf_op jit(solution)/shard_map/pallas_call | solution.py:148
  21.3 0.5 compare_select_fusion.refs_8_
  21.8 0.0 collective-permute-done.prev
  21.8 2.7 %convolution_convert_fusion.refs_5_ = bf16[128,1024]{1,0:T(8,128)(2,1)} fusion(bf16[128,1024]{1,0:T(8,128)(2,1)S(1)} %collective-permute-done.prev, bf16[1024,1024]{1,0:T(8,128)(2,1)} %param.10), kind=kOutput, calls=%fused_computation.3 | convolution fusion | flops 268566528 | bytes 2621440 | tf_op jit(solution)/shard_map/dot_general | solution.py:26
  24.6 0.0 copy-done.9
  24.6 1.2 convolution_convert_fusion.1.refs_4_
  25.8 0.6 broadcast_in_dim.21.total
  26.4 45.1 %shard_map.111 = (bf16[128,1024]{1,0:T(8,128)(2,1)}, f32[128,1024]{1,0:T(8,128)}, f32[128,1024]{1,0:T(8,128)}, f32[128,1024]{1,0:T(8,128)}, f32[128,1024]{1,0:T(...) custom-call(bf16[128,1024]{1,0:T(8,128)(2,1)} %shard_map.110.x, f32[8,1024]{1,0:T(8,128)} %broadcast_in_dim.21.total, ...), custom_call_target="tpu_custom_call" | custom-call | flops 1000000000 | bytes 100000000 | tf_op jit(solution)/shard_map/pallas_call | solution.py:283
  71.5 7.0 %shard_map.112 = (bf16[128,1024]{1,0:T(8,128)(2,1)}, bf16[128,1024]{1,0:T(8,128)(2,1)}, bf16[128,1024]{1,0:T(8,128)(2,1)}, bf16[128,1024]{1,0:T(8,128)(2,1)}) custom-call(bf16[128,1024]{1,0:T(8,128)(2,1)} %convolution_convert_fusion.4.q.refs_0_, bf16[128,1024]{1,0:T(8,128)(2,1)} %convolution_convert_fusion.3.k.refs_1_, ...), custom_call_target="tpu_custom_call" | custom-call | flops 1000000000 | bytes 10000000 | tf_op jit(solution)/shard_map/pallas_call | solution.py:170
  78.5 0.0 copy-start.4
  78.5 2.6 %fusion.3 = f32[128,1024]{1,0:T(8,128)S(1)} fusion(bf16[128,1024]{1,0:T(8,128)(2,1)} %get-tuple-element.25.dq, bf16[1024,1024]{1,0:T(8,128)(2,1)} %param.8), kind=kOutput, calls=%fused_computation.16 | convolution fusion | flops 268435456 | bytes 2883584 | tf_op jit(solution)/shard_map/dot_general | solution.py:26
  81.1 0.0 copy-start.2
  81.1 0.0 copy-start.8
  81.1 0.0 copy-done.4
  81.1 0.8 fusion.4
  82.0 0.0 copy-start.3
  82.0 0.0 copy-start.5
  82.0 0.0 copy-start.6
  82.0 0.1 copy-done.2
  82.1 0.7 copy-done.8
  82.8 0.8 fusion
  83.6 1.5 collective-permute-start.1
  85.1 0.0 copy-done.3
  85.1 0.0 copy-done.5
  85.1 0.0 copy-done.6
  85.1 80.8 %shard_map.113 = (bf16[128,8,1024]{2,1,0:T(8,128)(2,1)S(1)}, bf16[128,8,1024]{2,1,0:T(8,128)(2,1)S(1)}, bf16[128,8,1024]{2,1,0:T(8,128)(2,1)S(1)}) custom-call(bf16[128,1024]{1,0:T(8,128)(2,1)S(1)} %copy-done.1, bf16[128,1024]{1,0:T(8,128)(2,1)S(1)} %collective-permute-done.prev, bf16[128,1024]{1,0:T(8,128)(2,1)S(1)} %copy-done.6, ...), custom_call_target="tpu_custom_call" | custom-call | flops 1000000000 | bytes 100000000 | tf_op jit(solution)/shard_map/pallas_call | solution.py:397
  165.9 0.8 convolution_add_fusion.2
  166.8 0.0 collective-permute-done.1
  166.8 1.5 add_convert_fusion
  168.3 1.3 copy.17
  169.6 1.3 copy.18
  170.9 1.3 copy.19
Async XLA Ops:
  0.6 8.0 %copy-start = (bf16[1024,1024]{1,0:T(8,128)(2,1)S(1)}, bf16[1024,1024]{1,0:T(8,128)(2,1)}, u32[]{:S(2)}) copy-start(bf16[1024,1024]{1,0:T(8,128)(2,1)} %param.9) | copy-start | bytes 6291460
  0.6 8.0 %copy-start.1 = (bf16[128,1024]{1,0:T(8,128)(2,1)S(1)}, bf16[128,1024]{1,0:T(8,128)(2,1)}, u32[]{:S(2)}) copy-start(bf16[128,1024]{1,0:T(8,128)(2,1)} %tokens.1) | copy-start | bytes 786436
  0.7 21.2 %collective-permute-start = (bf16[128,1024]{1,0:T(8,128)(2,1)}, bf16[128,1024]{1,0:T(8,128)(2,1)S(1)}, u32[]{:S(2)}, u32[]{:S(2)}) collective-permute-start(bf16[128,1024]{1,0:T(8,128)(2,1)} %tokens.1), channel_id=1, source_target_pairs={{0,1},{1,2},{2,3},{3,4},{4,5},{5,6},{6,7},{7,8},{8,9},{9,10},{10,1... | collective-permute-start | bytes 786440 | tf_op jit(solution)/shard_map/ppermute | solution.py:22
  5.7 4.2 %copy-start.7 = (bf16[1024,1024]{1,0:T(8,128)(2,1)S(1)}, bf16[1024,1024]{1,0:T(8,128)(2,1)}, u32[]{:S(2)}) copy-start(bf16[1024,1024]{1,0:T(8,128)(2,1)} %param.10) | copy-start | bytes 6291460
  8.7 2.3 %copy-start.11 = (s32[1,4]{1,0:T(1,128)S(1)}, s32[1,4]{1,0:T(1,128)}, u32[]{:S(2)}) copy-start(s32[1,4]{1,0:T(1,128)} %param.12) | copy-start | bytes 52
  8.7 4.3 %copy-start.10 = (f32[16,128]{1,0:T(8,128)S(1)}, f32[16,128]{1,0:T(8,128)}, u32[]{:S(2)}) copy-start(f32[16,128]{1,0:T(8,128)} %param.11) | copy-start | bytes 24580
  13.2 11.4 %copy-start.9 = (f32[16,128]{1,0:T(8,128)}, f32[16,128]{1,0:T(8,128)S(1)}, u32[]{:S(2)}) copy-start(f32[16,128]{1,0:T(8,128)S(1)} %reduce_window_sum.11) | copy-start | bytes 24580
  78.5 2.6 %copy-start.4 = (bf16[128,1024]{1,0:T(8,128)(2,1)S(1)}, bf16[128,1024]{1,0:T(8,128)(2,1)}, u32[]{:S(2)}) copy-start(bf16[128,1024]{1,0:T(8,128)(2,1)} %get-tuple-element.28.pk) | copy-start | bytes 786436
  81.1 1.0 copy-start.2
  81.1 1.7 copy-start.8
  82.0 3.1 %copy-start.3 = (bf16[128,1024]{1,0:T(8,128)(2,1)S(1)}, bf16[128,1024]{1,0:T(8,128)(2,1)}, u32[]{:S(2)}) copy-start(bf16[128,1024]{1,0:T(8,128)(2,1)} %get-tuple-element.27.dv) | copy-start | bytes 786436
  82.0 3.1 %copy-start.5 = (bf16[128,1024]{1,0:T(8,128)(2,1)S(1)}, bf16[128,1024]{1,0:T(8,128)(2,1)}, u32[]{:S(2)}) copy-start(bf16[128,1024]{1,0:T(8,128)(2,1)} %get-tuple-element.26.dk) | copy-start | bytes 786436
  82.0 3.1 %copy-start.6 = (bf16[128,1024]{1,0:T(8,128)(2,1)S(1)}, bf16[128,1024]{1,0:T(8,128)(2,1)}, u32[]{:S(2)}) copy-start(bf16[128,1024]{1,0:T(8,128)(2,1)} %get-tuple-element.25.dq) | copy-start | bytes 786436
  83.6 83.1 %collective-permute-start.1 = (bf16[128,1024]{1,0:T(8,128)(2,1)S(1)}, bf16[128,1024]{1,0:T(8,128)(2,1)S(1)}, u32[]{:S(2)}, u32[]{:S(2)}) collective-permute-start(bf16[128,1024]{1,0:T(8,128)(2,1)S(1)} %fusion), channel_id=1, source_target_pairs={{1,0},{2,1},{3,2},{4,3},{5,4},{6,5},{7,6},{8,7},{9,8},{10,9},{11,1... | collective-permute-start | bytes 786440 | tf_op jit(solution)/shard_map/ppermute | solution.py:22

commit v4 on v3

--- a/solution.py
+++ b/solution.py
@@ -111,7 +111,7 @@
 
 def attention_parts(row_count, feat_width, head_count):
     size = feat_width // head_count
-    pair = 128 // size
+    pair = 256 // size
     steps = head_count // pair
     lanes = pair * size
     wide = pl.BlockSpec((row_count, lanes), lambda i: (0, i))
@@ -240,9 +240,10 @@
             sums[i] = log_all
             sent[i, :size, :] = tf.astype(BF16)
             sent[i, size:, :] = tb.astype(BF16)
+        rows = slice(None) if i + 1 < stages else pl.ds(pl.multiple_of(mine * size, size), size)
         copies = [
             pltpu.make_async_remote_copy(
-                src_ref=sent.at[i] if i else x, dst_ref=came.at[i],
+                src_ref=sent.at[i, rows] if i else x.at[rows], dst_ref=came.at[i, rows],
                 send_sem=sem.at[0, i], recv_sem=sem.at[1, i],
                 device_id=partner_of(bit), device_id_type=MESH,
             ),
@@ -258,6 +259,11 @@
         for copy in copies:
             copy.wait()
         log_other = sums_came[i]
+        if i + 1 == stages:
+            rows = pl.ds(pl.multiple_of((1 - mine) * size, size), size)
+            gap = jnp.where(jnp.full((1, width), mine) == 1, log_before[:1], log_after[:1])
+            carry[rows, :] += jnp.exp(gap) * came[i, rows, :].astype(F32)
+            break
         f_other = came[i, :size, :].astype(F32)
         b_other = came[i, size:, :].astype(F32)
         second = jnp.full((1, width), mine) == 1
@@ -266,12 +272,11 @@
         carry[size:, :] += jnp.where(second, 0.0, scale) * b_other
         log_before = log_before + jnp.where(second, log_other, 0.0)
         log_after = log_after + jnp.where(second, 0.0, log_other)
-        if i + 1 < stages:
-            here, there = jnp.exp(log_all[:1]), jnp.exp(log_other[:1])
-            one = jnp.ones_like(here)
-            tf = jnp.where(second, one, there) * tf + jnp.where(second, here, one) * f_other
-            tb = jnp.where(second, there, one) * tb + jnp.where(second, one, here) * b_other
-            log_all = log_all + log_other
+        here, there = jnp.exp(log_all[:1]), jnp.exp(log_other[:1])
+        one = jnp.ones_like(here)
+        tf = jnp.where(second, one, there) * tf + jnp.where(second, here, one) * f_other
+        tb = jnp.where(second, there, one) * tb + jnp.where(second, one, here) * b_other
+        log_all = log_all + log_other
     out[...] = carry[...].astype(BF16)
 
 

time: 173 us -> 166 us (0.960)
  Pallas kernels: 140 us -> 133 us
    pallas_call x1, Pallas kernels: 45.1 us -> 42.5 us  [carried(): pl.pallas_call(functools.partial(carry_kernel, bits, near, rows // 2), in...]
    pallas_call x1, Pallas kernels: 6.73 us -> 4.54 us  [shards(): pl.pallas_call(functools.partial(summary_kernel, lin_scale, size), grid=(...]
    pallas_call x1, Pallas kernels: 7.03 us -> 5.03 us  [shards(): pl.pallas_call(functools.partial(state_kernel, lin_scale, size), grid=(st...]
  transfers between devices with their start and end apart: 2 -> 2, of which waited for: 0 -> 0; matrix products, arithmetic and copies ran while one was open for 5% -> 5% of each run, Pallas kernels for 51% -> 52%
where the time goes in v4:
time: 166 us; the launch traced here: 165 us
  Pallas kernels  133 us (80%)
  matrix products  15.8 us (10%)
  local copies, waits for them, and re-layouts  6.6 us (4%)
  starting transfers between devices  6.31 us (4%)
  between operations  2.14 us (1%)
    pallas_call x1, Pallas kernels, reduce_grads(): pl.pallas_call(functools.partial(reduce_kernel, orders, norm), in_specs=[...  81 us
    pallas_call x1, Pallas kernels, carried(): pl.pallas_call(functools.partial(carry_kernel, bits, near, rows // 2), in...  42.5 us
    dot_general x10, matrix products, dot(): return lax.dot_general(a, b, dims, preferred_element_type=F32)  15.8 us
    ppermute x2, starting transfers between devices, shifted(): return lax.ppermute(block, axis, route)  6.31 us
    pallas_call x1, Pallas kernels, shards(): pl.pallas_call(functools.partial(state_kernel, lin_scale, size), grid=(st...  5.03 us
    unnamed x27, local copies, waits for them, and re-layouts  4.81 us
    pallas_call x1, Pallas kernels, shards(): pl.pallas_call(functools.partial(summary_kernel, lin_scale, size), grid=(...  4.54 us
  transfers between devices with their start and end apart: 2, of which 0 were waited for; matrix products, arithmetic and copies ran while one was open for 5% of the time, Pallas kernels for 52%

profile of v4, /device:TPU:0, one launch (start us, length us, event | category | flops | bytes accessed | tf_op | source)
XLA Modules:
  0.0 165.3 jit_solution(17565023580890659562)
XLA Ops:
  0.6 0.0 copy-start
  0.6 0.0 copy-start.1
  0.7 5.0 %collective-permute-start = (bf16[128,1024]{1,0:T(8,128)(2,1)}, bf16[128,1024]{1,0:T(8,128)(2,1)S(1)}, u32[]{:S(2)}, u32[]{:S(2)}) collective-permute-start(bf16[128,1024]{1,0:T(8,128)(2,1)} %tokens.1), channel_id=1, source_target_pairs={{0,1},{1,2},{2,3},{3,4},{4,5},{5,6},{6,7},{7,8},{8,9},{9,10},{10,1... | collective-permute-start | bytes 786440 | tf_op jit(solution)/shard_map/ppermute | solution.py:22
  5.7 0.0 copy-start.7
  5.7 3.0 %convolution_convert_fusion.4.q.refs_0_ = bf16[128,1024]{1,0:T(8,128)(2,1)} fusion(bf16[128,1024]{1,0:T(8,128)(2,1)} %tokens.1, bf16[1024,1024]{1,0:T(8,128)(2,1)} %param.8), kind=kOutput, calls=%fused_computation.7 | convolution fusion | flops 268566528 | bytes 2621440 | tf_op jit(solution)/shard_map/dot_general | solution.py:26
  8.7 0.0 copy-done
  8.7 0.0 copy-done.1
  8.7 0.0 copy-start.11
  8.7 0.0 copy-start.10
  8.7 1.2 convolution_convert_fusion.3.k.refs_1_
  9.8 0.0 copy-done.7
  9.8 1.2 convolution_convert_fusion.2.v.refs_2_
  11.0 0.0 copy-done.11
  11.0 0.6 fusion.1
  12.9 0.0 copy-done.10
  12.9 0.3 reduce_window_sum.11
  13.2 0.0 copy-start.9
  13.2 0.2 slice_reduce_fusion
  13.4 0.1 broadcast_in_dim.19
  13.5 0.1 broadcast_in_dim.20
  13.6 0.9 copy.13
  14.4 4.5 %shard_map.110.x = bf16[128,1024]{1,0:T(8,128)(2,1)} custom-call(bf16[128,1024]{1,0:T(8,128)(2,1)} %convolution_convert_fusion.4.q.refs_0_, bf16[128,1024]{1,0:T(8,128)(2,1)} %convolution_convert_fusion.3.k.refs_1_, bf16[128,1024]{1,0:T(8,128)(2,1)} %convolution_convert_fusion.2.v.refs_2_, bf16[128,1024]{1,0:T(8,128)(2,1)} %g.3, f32[4,128,4]{2,1,0:T(8,128)} %bitcast.28), custom_call_target="tpu_custom_call" | custom-call | flops 100000000 | bytes 1000000 | tf_op jit(solution)/shard_map/pallas_call | solution.py:148
  19.0 0.5 compare_select_fusion.refs_8_
  19.5 0.0 collective-permute-done.prev
  19.5 2.7 %convolution_convert_fusion.refs_5_ = bf16[128,1024]{1,0:T(8,128)(2,1)} fusion(bf16[128,1024]{1,0:T(8,128)(2,1)S(1)} %collective-permute-done.prev, bf16[1024,1024]{1,0:T(8,128)(2,1)} %param.10), kind=kOutput, calls=%fused_computation.3 | convolution fusion | flops 268566528 | bytes 2621440 | tf_op jit(solution)/shard_map/dot_general | solution.py:26
  22.2 0.0 copy-done.9
  22.2 1.2 convolution_convert_fusion.1.refs_4_
  23.4 0.6 broadcast_in_dim.21.total
  24.0 42.5 %shard_map.111 = (bf16[128,1024]{1,0:T(8,128)(2,1)}, f32[128,1024]{1,0:T(8,128)}, f32[128,1024]{1,0:T(8,128)}, f32[128,1024]{1,0:T(8,128)}, f32[128,1024]{1,0:T(...) custom-call(bf16[128,1024]{1,0:T(8,128)(2,1)} %shard_map.110.x, f32[8,1024]{1,0:T(8,128)} %broadcast_in_dim.21.total, ...), custom_call_target="tpu_custom_call" | custom-call | flops 1000000000 | bytes 100000000 | tf_op jit(solution)/shard_map/pallas_call | solution.py:288
  66.5 5.0 %shard_map.112 = (bf16[128,1024]{1,0:T(8,128)(2,1)}, bf16[128,1024]{1,0:T(8,128)(2,1)}, bf16[128,1024]{1,0:T(8,128)(2,1)}, bf16[128,1024]{1,0:T(8,128)(2,1)}) custom-call(bf16[128,1024]{1,0:T(8,128)(2,1)} %convolution_convert_fusion.4.q.refs_0_, bf16[128,1024]{1,0:T(8,128)(2,1)} %convolution_convert_fusion.3.k.refs_1_, ...), custom_call_target="tpu_custom_call" | custom-call | flops 1000000000 | bytes 10000000 | tf_op jit(solution)/shard_map/pallas_call | solution.py:170
  71.6 0.0 copy-start.4
  71.6 2.5 %fusion.3 = f32[128,1024]{1,0:T(8,128)S(1)} fusion(bf16[128,1024]{1,0:T(8,128)(2,1)} %get-tuple-element.25.dq, bf16[1024,1024]{1,0:T(8,128)(2,1)} %param.8), kind=kOutput, calls=%fused_computation.16 | convolution fusion | flops 268435456 | bytes 2883584 | tf_op jit(solution)/shard_map/dot_general | solution.py:26
  74.1 0.0 copy-start.2
  74.1 0.0 copy-start.8
  74.1 0.0 copy-done.4
  74.2 0.8 fusion.4
  75.0 0.0 copy-start.3
  75.0 0.0 copy-start.5
  75.0 0.0 copy-start.6
  75.0 0.1 copy-done.2
  75.1 0.7 copy-done.8
  75.8 0.8 fusion
  76.6 1.3 collective-permute-start.1
  77.9 0.0 copy-done.3
  78.0 0.0 copy-done.5
  78.0 0.0 copy-done.6
  78.0 81.0 %shard_map.113 = (bf16[128,8,1024]{2,1,0:T(8,128)(2,1)S(1)}, bf16[128,8,1024]{2,1,0:T(8,128)(2,1)S(1)}, bf16[128,8,1024]{2,1,0:T(8,128)(2,1)S(1)}) custom-call(bf16[128,1024]{1,0:T(8,128)(2,1)S(1)} %copy-done.1, bf16[128,1024]{1,0:T(8,128)(2,1)S(1)} %collective-permute-done.prev, bf16[128,1024]{1,0:T(8,128)(2,1)S(1)} %copy-done.6, ...), custom_call_target="tpu_custom_call" | custom-call | flops 1000000000 | bytes 100000000 | tf_op jit(solution)/shard_map/pallas_call | solution.py:402
  158.9 0.8 convolution_add_fusion.2
  159.8 0.0 collective-permute-done.1
  159.8 1.5 add_convert_fusion
  161.3 1.3 copy.17
  162.6 1.3 copy.18
  164.0 1.3 copy.19
Async XLA Ops:
  0.6 8.0 %copy-start = (bf16[1024,1024]{1,0:T(8,128)(2,1)S(1)}, bf16[1024,1024]{1,0:T(8,128)(2,1)}, u32[]{:S(2)}) copy-start(bf16[1024,1024]{1,0:T(8,128)(2,1)} %param.9) | copy-start | bytes 6291460
  0.6 8.0 %copy-start.1 = (bf16[128,1024]{1,0:T(8,128)(2,1)S(1)}, bf16[128,1024]{1,0:T(8,128)(2,1)}, u32[]{:S(2)}) copy-start(bf16[128,1024]{1,0:T(8,128)(2,1)} %tokens.1) | copy-start | bytes 786436
  0.7 18.8 %collective-permute-start = (bf16[128,1024]{1,0:T(8,128)(2,1)}, bf16[128,1024]{1,0:T(8,128)(2,1)S(1)}, u32[]{:S(2)}, u32[]{:S(2)}) collective-permute-start(bf16[128,1024]{1,0:T(8,128)(2,1)} %tokens.1), channel_id=1, source_target_pairs={{0,1},{1,2},{2,3},{3,4},{4,5},{5,6},{6,7},{7,8},{8,9},{9,10},{10,1... | collective-permute-start | bytes 786440 | tf_op jit(solution)/shard_map/ppermute | solution.py:22
  5.7 4.2 %copy-start.7 = (bf16[1024,1024]{1,0:T(8,128)(2,1)S(1)}, bf16[1024,1024]{1,0:T(8,128)(2,1)}, u32[]{:S(2)}) copy-start(bf16[1024,1024]{1,0:T(8,128)(2,1)} %param.10) | copy-start | bytes 6291460
  8.7 2.3 %copy-start.11 = (s32[1,4]{1,0:T(1,128)S(1)}, s32[1,4]{1,0:T(1,128)}, u32[]{:S(2)}) copy-start(s32[1,4]{1,0:T(1,128)} %param.12) | copy-start | bytes 52
  8.7 4.3 %copy-start.10 = (f32[16,128]{1,0:T(8,128)S(1)}, f32[16,128]{1,0:T(8,128)}, u32[]{:S(2)}) copy-start(f32[16,128]{1,0:T(8,128)} %param.11) | copy-start | bytes 24580
  13.2 9.0 %copy-start.9 = (f32[16,128]{1,0:T(8,128)}, f32[16,128]{1,0:T(8,128)S(1)}, u32[]{:S(2)}) copy-start(f32[16,128]{1,0:T(8,128)S(1)} %reduce_window_sum.11) | copy-start | bytes 24580
  71.6 2.6 %copy-start.4 = (bf16[128,1024]{1,0:T(8,128)(2,1)S(1)}, bf16[128,1024]{1,0:T(8,128)(2,1)}, u32[]{:S(2)}) copy-start(bf16[128,1024]{1,0:T(8,128)(2,1)} %get-tuple-element.28.pk) | copy-start | bytes 786436
  74.1 1.0 copy-start.2
  74.1 1.7 %copy-start.8 = (bf16[1024,1024]{1,0:T(8,128)(2,1)S(1)}, bf16[1024,1024]{1,0:T(8,128)(2,1)}, u32[]{:S(2)}) copy-start(bf16[1024,1024]{1,0:T(8,128)(2,1)} %param.10) | copy-start | bytes 6291460
  75.0 3.0 %copy-start.3 = (bf16[128,1024]{1,0:T(8,128)(2,1)S(1)}, bf16[128,1024]{1,0:T(8,128)(2,1)}, u32[]{:S(2)}) copy-start(bf16[128,1024]{1,0:T(8,128)(2,1)} %get-tuple-element.27.dv) | copy-start | bytes 786436
  75.0 3.0 %copy-start.5 = (bf16[128,1024]{1,0:T(8,128)(2,1)S(1)}, bf16[128,1024]{1,0:T(8,128)(2,1)}, u32[]{:S(2)}) copy-start(bf16[128,1024]{1,0:T(8,128)(2,1)} %get-tuple-element.26.dk) | copy-start | bytes 786436
  75.0 3.0 %copy-start.6 = (bf16[128,1024]{1,0:T(8,128)(2,1)S(1)}, bf16[128,1024]{1,0:T(8,128)(2,1)}, u32[]{:S(2)}) copy-start(bf16[128,1024]{1,0:T(8,128)(2,1)} %get-tuple-element.25.dq) | copy-start | bytes 786436
  76.6 83.1 %collective-permute-start.1 = (bf16[128,1024]{1,0:T(8,128)(2,1)S(1)}, bf16[128,1024]{1,0:T(8,128)(2,1)S(1)}, u32[]{:S(2)}, u32[]{:S(2)}) collective-permute-start(bf16[128,1024]{1,0:T(8,128)(2,1)S(1)} %fusion), channel_id=1, source_target_pairs={{1,0},{2,1},{3,2},{4,3},{5,4},{6,5},{7,6},{8,7},{9,8},{10,9},{11,1... | collective-permute-start | bytes 786440 | tf_op jit(solution)/shard_map/ppermute | solution.py:22
